TPU v7x, 512 devices: a whole 4x4x16 slice. The times are simulated.
512 devices in a mesh: row: 8 (over x, y_lo), col: 32 (over y_hi, z), img: 2 (over core).
Axes of the slice: x: 4, y: 4 (y_hi: 2, y_lo: 2; y = y_hi * 2 + y_lo), z: 16, core: 2. Of those that a mesh axis runs over, the one named last changes fastest.
Arguments:
- x_in: bfloat16 [2, 256, 256, 1536], P('img', 'row', 'col'), may hold values from -6 to 6
- gate_in: bfloat16 [2, 256, 256, 1536], P('img', 'row', 'col'), may hold values from -6 to 6
- proj_bc: bfloat16 [2, 256, 256, 64], P('img', 'row', 'col'), may hold values from -3 to 3
- dt_raw: bfloat16 [2, 256, 256, 48], P('img', 'row', 'col'), may hold values from -3 to 3
- step_index: int32 [2], P('img'), may hold values from 0 to 999
- step_table: float32 [1000, 48], replicated, may hold values from -1.5 to 0.5
- rates: float32 [2, 24], replicated, may hold values from 0.000390625 to 0.046875, as said below
- skip: float32 [24], replicated, may hold values from 0.5 to 2
- norm_gain: float32 [1536], replicated, may hold values from 0.5 to 1.5
Outputs:
- mixed: bfloat16 [2, 256, 256, 1536], P('img', 'row', 'col')
Inputs may be any that keep to these rules, and one draw needn't show every extreme that they name: rates of the row heads are given per column step and those of the column heads per row step.
All inputs are finite; a program needn't handle non-finite values.
Results may differ from a plain program's by a relative error of at most 0.0065.
Values may be sent and summed in bfloat16 or wider, within the bound.
A program may use at most 128 MiB of HBM per device.

v0:
```python
import jax
import jax.numpy as jnp
from jax import lax
from jax.sharding import PartitionSpec as P

SPAN = 64


def prefix(part, axis, combine, identity):
    place = lax.axis_index(axis)
    gathered = jax.tree.map(lambda a: lax.all_gather(a, axis), part)
    state = jax.tree.map(lambda a, e: jnp.zeros_like(a) + jnp.asarray(e, a.dtype), part, identity)

    def one(turn, state):
        return combine(
            state, jax.tree.map(lambda a: lax.dynamic_index_in_dim(a, turn, 0, False), gathered)
        )

    return lax.fori_loop(0, place, one, state)


def segment_scan(inputs, decay_log, in_map, out_map):
    line_count, length, heads, width = inputs.shape
    block = min(SPAN, length)
    blocks = length // block
    values = inputs.astype(jnp.float32).reshape(line_count, blocks, block, heads, width)
    running = jnp.cumsum(decay_log.reshape(line_count, blocks, block, heads), axis=2)
    b_block = in_map.reshape(line_count, blocks, block, -1)
    c_block = out_map.reshape(line_count, blocks, block, -1)
    scores = jnp.einsum("lkin,lkjn->lkij", c_block, b_block, preferred_element_type=jnp.float32)
    spacing = running[:, :, :, None, :] - running[:, :, None, :, :]
    positions = jnp.arange(block)
    lower = (positions[:, None] >= positions[None, :])[None, None, :, :, None]
    weights = jnp.where(lower, jnp.exp(jnp.where(lower, spacing, 0.0)), 0.0) * scores[..., None]
    within = jnp.einsum("lkijh,lkjhp->lkihp", weights, values, precision=lax.Precision.HIGHEST)
    to_end = jnp.exp(running[:, :, -1:, :] - running)
    b_float = b_block.astype(jnp.float32)
    c_float = c_block.astype(jnp.float32)
    block_states = jnp.einsum(
        "lkjh,lkjhp,lkjn->lkhpn", to_end, values, b_float, precision=lax.Precision.HIGHEST
    )
    block_ends = running[:, :, -1, :]

    def advance(carry, items):
        state_now, total_now = carry
        block_state, block_end = items
        state_next = jnp.exp(block_end)[..., None, None] * state_now + block_state
        return ((state_next, total_now + block_end), (state_now, total_now))

    start = (
        jnp.zeros((line_count, heads, width, b_block.shape[-1]), jnp.float32),
        jnp.zeros((line_count, heads), jnp.float32),
    )
    (final, total), (before, offsets) = lax.scan(
        advance, start, (jnp.moveaxis(block_states, 1, 0), jnp.moveaxis(block_ends, 1, 0))
    )
    before = jnp.moveaxis(before, 0, 1)
    offsets = jnp.moveaxis(offsets, 0, 1)
    carried = jnp.exp(running)[..., None] * jnp.einsum(
        "lkin,lkhpn->lkihp", c_float, before, precision=lax.Precision.HIGHEST
    )
    outputs = (within + carried).reshape(line_count, length, heads, width)
    whole_running = (running + offsets[:, :, None, :]).reshape(line_count, length, heads)
    return (outputs, final, total, whole_running)


def prepare(tokens, raw_steps, line_bias, rate):
    line_count, length, channels = tokens.shape
    heads = raw_steps.shape[-1]
    step_size = jax.nn.softplus(raw_steps.astype(jnp.float32) + line_bias[:, None, :])
    decay_log = -rate * step_size
    scaled = (
        step_size[..., None]
        * tokens.astype(jnp.float32).reshape(line_count, length, heads, channels // heads)
    ).astype(jnp.bfloat16)
    return (scaled, decay_log)


def run_lines(tokens, raw_steps, maps, line_bias, rate):
    line_count, length, channels = tokens.shape
    state = maps.shape[-1] // 2
    scaled, decay_log = prepare(tokens, raw_steps, line_bias, rate)
    outputs, final, total, whole_running = segment_scan(
        scaled, decay_log, maps[..., :state], maps[..., state:]
    )
    return outputs.astype(jnp.bfloat16).reshape(line_count, length, channels)


def join_states(earlier, later):
    total_early, state_early = earlier
    total_late, state_late = later
    return (
        total_early + total_late,
        jnp.exp(total_late)[..., None, None] * state_early + state_late,
    )


def body(x_in, gate_in, proj_bc, dt_raw, step_index, step_table, rates, skip, norm_gain):
    images, tile_rows, tile_cols, channels = x_in.shape
    heads = skip.shape[0]
    width = channels // heads
    state = proj_bc.shape[-1] // 4
    onehot = (jnp.arange(step_table.shape[0])[None, :] == step_index[:, None]).astype(jnp.float32)
    image_bias = jnp.dot(
        onehot, step_table, precision=lax.Precision.HIGHEST, preferred_element_type=jnp.float32
    )
    row_lines = images * tile_rows
    sent_rows = (
        x_in.reshape(row_lines, tile_cols, channels),
        dt_raw[..., :heads].reshape(row_lines, tile_cols, heads),
        proj_bc[..., : 2 * state].reshape(row_lines, tile_cols, 2 * state),
    )
    got_tokens, got_steps, got_maps = (
        lax.all_to_all(sent_rows[0], "col", split_axis=0, concat_axis=1, tiled=True),
        lax.all_to_all(sent_rows[1], "col", split_axis=0, concat_axis=1, tiled=True),
        lax.all_to_all(sent_rows[2], "col", split_axis=0, concat_axis=1, tiled=True),
    )
    per_device = got_tokens.shape[0]
    row_bias = lax.dynamic_slice_in_dim(
        jnp.repeat(image_bias[:, :heads], tile_rows, axis=0),
        lax.axis_index("col") * per_device,
        per_device,
        0,
    )
    row_result = run_lines(got_tokens, got_steps, got_maps, row_bias, rates[0])
    y_row = lax.all_to_all(row_result, "col", split_axis=1, concat_axis=0, tiled=True).reshape(
        images, tile_rows, tile_cols, heads, width
    )
    col_lines = images * tile_cols
    col_tokens = jnp.swapaxes(x_in, 1, 2).reshape(col_lines, tile_rows, channels)
    col_steps = jnp.swapaxes(dt_raw[..., heads:], 1, 2).reshape(col_lines, tile_rows, heads)
    col_maps = jnp.swapaxes(proj_bc[..., 2 * state :], 1, 2).reshape(
        col_lines, tile_rows, 2 * state
    )
    col_bias_all = jnp.repeat(image_bias[:, heads:], tile_cols, axis=0)
    scaled, decay_log = prepare(col_tokens, col_steps, col_bias_all, rates[1])
    outputs, final, total, whole_running = segment_scan(
        scaled, decay_log, col_maps[..., :state], col_maps[..., state:]
    )
    total_in, state_in = prefix(
        (total, final), "row", join_states, (jnp.zeros_like(total), jnp.zeros_like(final))
    )
    entering = jnp.einsum(
        "lsn,lhpn->lshp",
        col_maps[..., state:].astype(jnp.float32),
        state_in,
        precision=lax.Precision.HIGHEST,
    )
    outputs = outputs + jnp.exp(whole_running)[..., None] * entering
    y_col_lines = outputs.astype(jnp.bfloat16).reshape(col_lines, tile_rows, channels)
    y_col = jnp.swapaxes(y_col_lines.reshape(images, tile_cols, tile_rows, heads, width), 1, 2)
    x_heads = x_in.astype(jnp.float32).reshape(images, tile_rows, tile_cols, heads, width)
    gate = jax.nn.silu(
        gate_in.astype(jnp.float32).reshape(images, tile_rows, tile_cols, heads, width)
    )
    mixed = (y_row.astype(jnp.float32) + y_col.astype(jnp.float32) + skip[:, None] * x_heads) * gate
    power = jnp.mean(mixed * mixed, axis=(-2, -1), keepdims=True)
    normed = mixed * lax.rsqrt(power + 1e-05) * norm_gain.reshape(heads, width)
    return normed.astype(jnp.bfloat16).reshape(images, tile_rows, tile_cols, channels)


def solution(mesh):
    return jax.shard_map(
        body,
        mesh=mesh,
        in_specs=(
            P("img", "row", "col", None),
            P("img", "row", "col", None),
            P("img", "row", "col", None),
            P("img", "row", "col", None),
            P("img"),
            P(),
            P(),
            P(),
            P(),
        ),
        out_specs=P("img", "row", "col", None),
        check_vma=False,
    )
```

profile of v0, /device:TPU:6, one launch (start us, length us, event | category | flops | bytes accessed | tf_op | source)
XLA Modules:
  0.0 342.8 jit_solution(1473881480287602453)
XLA Ops:
  10.7 1.9 fusion.82
  14.0 1.6 fusion.80
  17.7 2.5 convert_bitcast_fusion.1
  20.3 2.4 reshape.575
  22.7 6.1 %fusion.36 = f32[8,24,64,16]{2,3,1,0:T(8,128)} fusion(f32[8,32,16]{1,2,0:T(8,128)} %slice_convert_fusion, f32[8,32,24]{1,2,0:T(8,128)S(1)} %copy-done.5, f32[8,24]{1,0:T(8,128)S(1)} %exponential_multiply_fusion, f32[8,32,24,64]{3,2,0,1:T(8,128)S(1)} %reshape.575, f32[8,32,24]{1,2,0:T(8,128)S(1)} %copy-done.6), kind=kOutput, calls=%fused_computation.53 | convolution fusion | flops 76578816 | bytes 2425600 | tf_op jit(solution)/shard_map/lkjh,lkjhp,lkjn->lkhpn/dot_general | solution.py:39
  28.9 18.1 %all-to-all-start = ((bf16[32,8,24]{2,1,0:T(8,128)(2,1)}), bf16[32,8,24]{2,1,0:T(8,128)(2,1)S(1)}, u32[]{:S(2)}, u32[]{:S(2)}) async-start(bf16[32,8,24]{2,1,0:T(8,128)(2,1)} %get-tuple-element.173), calls=%async_computation | async-start | bytes 131072 | tf_op jit(solution)/shard_map/all_to_all | solution.py:115
  48.0 14.9 %all-to-all-done = bf16[32,8,24]{2,1,0:T(8,128)(2,1)S(1)} async-done(((bf16[32,8,24]{2,1,0:T(8,128)(2,1)}), bf16[32,8,24]{2,1,0:T(8,128)(2,1)S(1)}, u32[]{:S(2)}, u32[]{:S(2)}) %all-to-all-start) | async-done | bytes 12320 | tf_op jit(solution)/shard_map/all_to_all | solution.py:115
  62.9 17.9 %all_to_all.19 = bf16[32,2,128]{2,1,0:T(2,128)(2,1)S(1)} all-to-all(bf16[32,2,128]{2,1,0:T(2,128)(2,1)S(1)} %reshape.589), channel_id=1, replica_groups=mesh['row'=8,'col'=32,'img'=2] {'col'}, dimensions={0} | all-to-all | bytes 32768 | tf_op jit(solution)/shard_map/all_to_all | solution.py:116
  80.8 4.8 %all-to-all-start.1 = ((bf16[32,8,1536]{2,1,0:T(8,128)(2,1)}), bf16[32,8,1536]{2,1,0:T(8,128)(2,1)}, u32[]{:S(2)}, u32[]{:S(2)}) async-start(bf16[32,8,1536]{2,1,0:T(8,128)(2,1)} %bitcast.221), calls=%async_computation.1 | async-start | bytes 1572864 | tf_op jit(solution)/shard_map/all_to_all | solution.py:114
  89.1 1.6 copy.111
  90.7 1.7 fusion.52
  92.3 1.7 reduce_window_sum.22
  94.0 1.6 copy.113
  96.9 1.7 subtract_exponential_fusion.1
  98.5 1.6 copy.121
  100.2 1.6 copy.120
  102.5 1.7 slice_convert_fusion.1
  104.1 1.6 copy.122
  106.7 1.7 fusion.84
  108.4 18.3 %all-to-all-done.1 = bf16[32,8,1536]{2,1,0:T(8,128)(2,1)} async-done(((bf16[32,8,1536]{2,1,0:T(8,128)(2,1)}), bf16[32,8,1536]{2,1,0:T(8,128)(2,1)}, u32[]{:S(2)}, u32[]{:S(2)}) %all-to-all-start.1) | async-done | bytes 786464 | tf_op jit(solution)/shard_map/all_to_all | solution.py:114
  126.6 3.3 reshape.571
  130.0 4.8 %convolution_bitcast_fusion = f32[4,1,24,64,16]{3,4,2,1,0:T(8,128)} fusion(f32[4,64,16]{1,2,0:T(8,128)} %copy.122, f32[4,64,24]{1,2,0:T(8,128)} %copy.121, f32[4,64,24,64]{3,2,1,0:T(8,128)} %reshape.571, f32[4,64,24]{1,2,0:T(8,128)} %copy.111), kind=kOutput, calls=%fused_computation.54 | convolution fusion | flops 76382208 | bytes 2031616 | tf_op jit(solution)/shard_map/lkjh,lkjhp,lkjn->lkhpn/dot_general | solution.py:39
  134.8 6.5 %fusion.17 = f32[4,24,64,64]{3,2,1,0:T(8,128)} fusion(f32[4,64,64]{2,1,0:T(8,128)S(1)} %copy-done.10, f32[4,64,24]{1,2,0:T(8,128)S(1)} %copy-done.12, pred[64,64]{1,0:T(8,128)(4,1)S(1)} %copy-done.15, f32[4,64,24,64]{3,2,1,0:T(8,128)S(1)} %copy-done.2, f32[4,64,24]{1,2,0:T(8,128)S(1)} %copy-done.9), kind=kOutput, calls=%fused_computation.33 | convolution fusion | flops 304349184 | bytes 3264512 | tf_op jit(solution)/shard_map/lkijh,lkjhp->lkihp/dot_general | solution.py:35
  141.3 9.4 %while.8 = (s32[]{:T(128)}, f32[1,24,64,16]{2,3,1,0:T(8,128)S(1)}, f32[4,1,24,64,16]{3,4,2,1,0:T(8,128)}, f32[4,1,24]{2,1,0:T(1,128)}, f32[4,1,24,64,16]{3,4,2,1,0:T(8,128)}, /*index=5*/s32[]{:T(128)}, s32[]{:T(128)}) while((s32[]{:T(128)}, f32[1,24,64,16]{2,3,1,0:T(8,128)S(1)}, f32[4,1,24,64,16]{3,4,2,1,0:T(8,128)}, ...), condition=%wide.region_2.3_spmd.clone, body=%wide.region_1.2_spmd.clone.sunk | while | flops 98307 | bytes 590220 | solution.py:54
  150.7 6.0 %fusion.8 = bf16[1,4,64,24,64]{2,4,3,1,0:T(8,128)(2,1)} fusion(f32[4,24,64,64]{3,2,1,0:T(8,128)} %fusion.17, f32[4,64,24]{1,2,0:T(8,128)} %copy.120, f32[4,1,24,64,16]{3,4,2,1,0:T(8,128)} %get-tuple-element.97, bf16[4,64,16,1]{1,0,2,3:T(4,128)(2,1)S(1)} %bitcast.238), kind=kOutput, calls=%fused_computation.16 | convolution fusion | flops 76677120 | bytes 2785280 | tf_op jit(solution)/shard_map/lkin,lkhpn->lkihp/dot_general | solution.py:59
  156.7 2.8 copy.126
  159.5 6.4 %convert_element_type.182 = bf16[1,256,1536]{2,0,1:T(2,128)(2,1)} reshape(bf16[1,4,64,24,64]{4,3,2,1,0:T(8,128)(2,1)} %copy.126) | data formatting | bytes 1572864 | tf_op jit(solution)/shard_map/convert_element_type | solution.py:86
  166.4 7.3 %reduce.3 = bf16[256,1536]{1,0:T(8,128)(2,1)} reduce(bf16[256,1,1536]{2,1,0:T(2,128)(2,1)} %bitcast.222, bf16[]{:T(256)} %broadcast.268), dimensions={1}, to_apply=%bitcast.198.reduce_sub_computation | reduce | bytes 1572866
  173.7 3.2 reshape.591
  176.8 6.4 %all-to-all-start.3 = ((bf16[32,2,6144]{2,1,0:T(2,128)(2,1)}), bf16[32,2,6144]{2,1,0:T(2,128)(2,1)}, u32[]{:S(2)}, u32[]{:S(2)}) async-start(bf16[32,2,6144]{2,1,0:T(2,128)(2,1)} %reshape.591), calls=%async_computation.3 | async-start | bytes 1572864 | tf_op jit(solution)/shard_map/all_to_all | solution.py:126
  183.3 3.3 reshape.578
  187.5 3.3 reshape.580
  190.8 41.1 %all-gather = f32[64,1,1,24]{3,0,1,2:T(8,128)} all-gather(f32[8,1,1,24]{3,0,1,2:T(8,128)S(1)} %copy-done.13), channel_id=2, replica_groups=mesh['row'=8,'col'=32,'img'=2] {'row'}, dimensions={0}, use_global_device_ids=true | all-gather | bytes 6912 | tf_op jit(solution)/shard_map/all_gather | solution.py:11
  232.1 2.5 fusion.43
  234.6 6.1 %fusion.11 = f32[8,24,64,32]{2,3,1,0:T(8,128)} fusion(f32[8,32,32]{2,1,0:T(8,128)S(1)} %fusion.70, f32[8,32,24]{1,2,0:T(8,128)S(1)} %copy-done.11, pred[32,32]{1,0:T(8,128)(4,1)S(1)} %iota_compare_fusion.1, f32[8,32,24,64]{3,2,0,1:T(8,128)S(1)} %reshape.575, f32[8,32,24]{1,2,0:T(8,128)S(1)} %copy-done.7), kind=kOutput, calls=%fused_computation.27 | convolution fusion | flops 152567808 | bytes 3228672 | tf_op jit(solution)/shard_map/lkijh,lkjhp->lkihp/dot_general | solution.py:35
  240.7 4.9 %reshape.592 = bf16[256,1,1536]{2,1,0:T(2,128)(2,1)S(1)} reshape(bf16[32,2,6144]{2,1,0:T(2,128)(2,1)} %all-to-all-done.3) | data formatting | bytes 1572864
  245.6 4.5 %convert_reduce_fusion = f32[256,1536]{1,0:T(8,128)S(1)} fusion(bf16[256,1,1536]{2,1,0:T(2,128)(2,1)S(1)} %reshape.592), kind=kLoop, calls=%fused_computation.41 | loop fusion | flops 393216 | bytes 2359296 | tf_op jit(solution)/shard_map/convert_element_type | solution.py:156
  250.2 2.1 reshape.573
  252.2 54.0 %all-gather.4.cloned.1.call-done = f32[64,24,64,16]{2,3,1,0:T(8,128)} async-done(((f32[8,24,64,16]{2,3,1,0:T(8,128)}), f32[64,24,64,16]{2,3,1,0:T(8,128)}) %all-gather.4.cloned.1.call-update) | async-done | bytes 6291472 | tf_op jit(solution)/shard_map/all_gather | solution.py:11
  306.4 15.0 %while.7 = (s32[]{:T(128)}, f32[8,24,64,16]{2,3,1,0:T(8,128)S(1)}, s32[]{:T(128)}, f32[8,8,24]{2,1,0:T(8,128)}, f32[8,8,24,64,16]{3,4,2,1,0:T(8,128)}, /*index=5*/s32[]{:T(128)}, s32[]{:T(128)}, s32[]{:T(128)}) while((s32[]{:T(128)}, f32[8,24,64,16]{2,3,1,0:T(8,128)S(1)}, s32[]{:T(128)}, f32[8,8,24]{2,1,0:T(8,128)}, ...), condition=%wide.region_5.6_spmd, body=%wide.region_4.5_spmd.sunk | while | flops 393221 | bytes 2361735 | solution.py:19
  307.1 1.8 bitcast_add_fusion.7
  309.6 1.8 bitcast_add_fusion.7
  312.1 1.8 bitcast_add_fusion.7
  314.6 1.8 bitcast_add_fusion.7
  317.1 1.8 bitcast_add_fusion.7
  319.6 1.8 bitcast_add_fusion.7
  321.4 11.7 %multiply_reduce_fusion = (f32[32,8]{0,1:T(8,128)S(1)}, f32[1,32,8,24,64]{4,1,3,2,0:T(8,128)S(1)}) fusion(f32[1,32,8,24,64]{4,3,2,1,0:T(8,128)} %reshape.580, f32[1,32,8,24,64]{4,3,2,1,0:T(8,128)} %reshape.578, f32[24]{0:T(128)S(1)} %copy-done.16, f32[8,24,64,16]{2,3,1,0:T(8,128)S(1)} %get-tuple-element.98, bf16[8,32,32]{1,2,0:T(8,128)(2,1)S(1)} %bitcast.231, ...), kind=kOutput, calls=%fused_computation.26 | convolution fusion | flops 81788672 | bytes 11142656 | tf_op jit(solution)/shard_map/lsn,lhpn->lshp/dot_general | solution.py:143
  334.3 1.7 reshape.569
  (89 shorter events, 30.8 us)
Async XLA Ops:
  6.5 2.4 copy-start
  6.5 299.7 %all-gather.4.cloned.1.call-start = ((), (), s32[]{:S(2)}) async-start(), calls=%async_computation.4 | async-start | bytes 14155776 | tf_op jit(solution)/shard_map/all_gather | solution.py:11
  17.7 5.0 %copy-start.5 = (f32[8,32,24]{1,2,0:T(8,128)S(1)}, f32[8,32,24]{1,2,0:T(8,128)}, u32[]{:S(2)}) copy-start(f32[8,32,24]{1,2,0:T(8,128)} %copy.135) | copy-start | bytes 73732
  17.7 5.0 %copy-start.6 = (f32[8,32,24]{1,2,0:T(8,128)S(1)}, f32[8,32,24]{1,2,0:T(8,128)}, u32[]{:S(2)}) copy-start(f32[8,32,24]{1,2,0:T(8,128)} %compare_select_fusion.3) | copy-start | bytes 73732
  28.9 34.0 %all-to-all-start = ((bf16[32,8,24]{2,1,0:T(8,128)(2,1)}), bf16[32,8,24]{2,1,0:T(8,128)(2,1)S(1)}, u32[]{:S(2)}, u32[]{:S(2)}) async-start(bf16[32,8,24]{2,1,0:T(8,128)(2,1)} %get-tuple-element.173), calls=%async_computation | async-start | bytes 131072 | tf_op jit(solution)/shard_map/all_to_all | solution.py:115
  62.8 17.9 %copy-start.8 = (bf16[32,8,24]{2,1,0:T(8,128)(2,1)}, bf16[32,8,24]{2,1,0:T(8,128)(2,1)S(1)}, u32[]{:S(2)}) copy-start(bf16[32,8,24]{2,1,0:T(8,128)(2,1)S(1)} %all-to-all-done) | copy-start | bytes 36868
  80.8 45.9 %all-to-all-start.1 = ((bf16[32,8,1536]{2,1,0:T(8,128)(2,1)}), bf16[32,8,1536]{2,1,0:T(8,128)(2,1)}, u32[]{:S(2)}, u32[]{:S(2)}) async-start(bf16[32,8,1536]{2,1,0:T(8,128)(2,1)} %bitcast.221), calls=%async_computation.1 | async-start | bytes 1572864 | tf_op jit(solution)/shard_map/all_to_all | solution.py:114
  87.0 0.7 copy-start.3
  129.9 4.8 %copy-start.2 = (f32[4,64,24,64]{3,2,1,0:T(8,128)S(1)}, f32[4,64,24,64]{3,2,1,0:T(8,128)}, u32[]{:S(2)}) copy-start(f32[4,64,24,64]{3,2,1,0:T(8,128)} %reshape.571) | copy-start | bytes 4718596
  129.9 4.8 %copy-start.9 = (f32[4,64,24]{1,2,0:T(8,128)S(1)}, f32[4,64,24]{1,2,0:T(8,128)}, u32[]{:S(2)}) copy-start(f32[4,64,24]{1,2,0:T(8,128)} %copy.111) | copy-start | bytes 73732
  129.9 4.8 %copy-start.10 = (f32[4,64,64]{2,1,0:T(8,128)S(1)}, f32[4,64,64]{2,1,0:T(8,128)}, u32[]{:S(2)}) copy-start(f32[4,64,64]{2,1,0:T(8,128)} %fusion.84) | copy-start | bytes 196612
  129.9 4.8 %copy-start.12 = (f32[4,64,24]{1,2,0:T(8,128)S(1)}, f32[4,64,24]{1,2,0:T(8,128)}, u32[]{:S(2)}) copy-start(f32[4,64,24]{1,2,0:T(8,128)} %copy.113) | copy-start | bytes 73732
  129.9 4.8 %copy-start.15 = (pred[64,64]{1,0:T(8,128)(4,1)S(1)}, pred[64,64]{1,0:T(8,128)(4,1)}, u32[]{:S(2)}) copy-start(pred[64,64]{1,0:T(8,128)(4,1)} %iota_compare_fusion) | copy-start | bytes 12292
  176.8 9.7 %copy-start.14 = (f32[1536]{0:T(1024)S(1)}, f32[1536]{0:T(1024)}, u32[]{:S(2)}) copy-start(f32[1536]{0:T(1024)} %param.21) | copy-start | bytes 18436
  176.8 10.5 %copy-start.4 = (f32[8,32,24]{2,0,1:T(8,128)S(1)}, f32[8,32,24]{2,0,1:T(8,128)}, u32[]{:S(2)}) copy-start(f32[8,32,24]{2,0,1:T(8,128)} %get-tuple-element.162) | copy-start | bytes 73732
  176.8 63.9 %all-to-all-start.3 = ((bf16[32,2,6144]{2,1,0:T(2,128)(2,1)}), bf16[32,2,6144]{2,1,0:T(2,128)(2,1)}, u32[]{:S(2)}, u32[]{:S(2)}) async-start(bf16[32,2,6144]{2,1,0:T(2,128)(2,1)} %reshape.591), calls=%async_computation.3 | async-start | bytes 1572864 | tf_op jit(solution)/shard_map/all_to_all | solution.py:126
  186.6 4.2 %copy-start.13 = (f32[8,1,1,24]{3,0,1,2:T(8,128)S(1)}, f32[8,1,1,24]{3,0,1,2:T(8,128)}, u32[]{:S(2)}) copy-start(f32[8,1,1,24]{3,0,1,2:T(8,128)} %get-tuple-element.165) | copy-start | bytes 2308
  187.5 47.1 %copy-start.7 = (f32[8,32,24]{1,2,0:T(8,128)S(1)}, f32[8,32,24]{1,2,0:T(8,128)}, u32[]{:S(2)}) copy-start(f32[8,32,24]{1,2,0:T(8,128)} %compare_select_fusion.3) | copy-start | bytes 73732
  190.8 43.8 %copy-start.11 = (f32[8,32,24]{1,2,0:T(8,128)S(1)}, f32[8,32,24]{1,2,0:T(8,128)}, u32[]{:S(2)}) copy-start(f32[8,32,24]{1,2,0:T(8,128)} %copy.131) | copy-start | bytes 73732
  306.4 15.1 %copy-start.16 = (f32[24]{0:T(128)S(1)}, f32[24]{0:T(128)}, u32[]{:S(2)}) copy-start(f32[24]{0:T(128)} %param.20) | copy-start | bytes 292
  333.1 2.8 copy-start.1
Sparse Core Ops, SparseCore 0:
  29.0 277.1 all-gather.3
where the time goes:
time: 347 us; the launch traced here: 343 us
  waiting for transfers between devices  87.2 us (25%)
  local copies, waits for them, and re-layouts  59.5 us (17%)
  blocking collectives  59 us (17%)
  other arithmetic  47.5 us (14%)
  matrix products  45.8 us (13%)
  starting transfers between devices  29.3 us (8%)
  between operations  14.4 us (4%)
    all_gather x1, waiting for transfers between devices, prefix(): gathered = jax.tree.map(lambda a: lax.all_gather(a, axis), part)  54 us
    all_gather x1, blocking collectives, prefix(): gathered = jax.tree.map(lambda a: lax.all_gather(a, axis), part)  41.1 us
    all_to_all x1, waiting for transfers between devices, body(): lax.all_to_all(sent_rows[0], 'col', split_axis=0, concat_axis=1, tiled=True)  18.3 us
    all_to_all x1, starting transfers between devices, body(): lax.all_to_all(sent_rows[1], 'col', split_axis=0, concat_axis=1, tiled=True)  18.1 us
    all_to_all x1, blocking collectives, body(): lax.all_to_all(sent_rows[2], 'col', split_axis=0, concat_axis=1, tiled=True)  17.9 us
    all_to_all x1, waiting for transfers between devices, body(): lax.all_to_all(sent_rows[1], 'col', split_axis=0, concat_axis=1, tiled=True)  14.9 us
    dot_general x2, matrix products, segment_scan(): jnp.einsum('lkijh,lkjhp->lkihp', weights, values, precision=lax.Precision...  12.6 us
    dot_general x1, matrix products, body(): jnp.einsum('lsn,lhpn->lshp', col_maps[..., state:].astype(jnp.float32), s...  11.7 us
  transfers between devices with their start and end apart: 4, of which 3 were waited for; matrix products, arithmetic and copies ran while one was open for 29% of the time, Pallas kernels for 0%

commit v1 on v0

v1 whole, which is shorter than its diff:
```python
import functools

import jax
import jax.numpy as jnp
from jax import lax
from jax.experimental import pallas as pl
from jax.experimental.pallas import tpu as pltpu
from jax.sharding import PartitionSpec as P

HEADS = 24
HEAD = 64
STATE = 16
INNER = HEADS * HEAD
GROUPS = 4
LOG2E = 1.4426950408889634
F32 = jnp.float32
BF16 = jnp.bfloat16


def dot(a, b):
    return jnp.dot(a, b, preferred_element_type=F32)


def split(v, pieces):
    parts = []
    for _ in range(pieces):
        part = v.astype(BF16)
        parts.append(part)
        v = v - part.astype(F32)
    return parts


def dot_exact(zero_one, v, pieces=3):
    return sum(dot(zero_one, part) for part in split(v, pieces))


def expand(v, heads_to_channels, pieces=2):
    return sum(dot(part, heads_to_channels) for part in split(v, pieces))


def softplus(v):
    return jnp.maximum(v, 0.0) + jnp.log(1.0 + jnp.exp(-jnp.abs(v)))


def kernel(
    lanes, tall, step_ref, table_ref, rates_ref, skip_ref, gain_ref, x_ref, gate_ref, bc_ref, dt_ref, out_ref,
    got_x, got_bc, got_dt, y_send, got_y, f_send, got_f, t_send, got_t, s_send, got_s, w_row, u_row_s, acc, act, mixed,
    x_out, x_in, m_out, m_in, y_out, y_in, f_out, f_in, s_out, s_in,
):
    tokens = lanes * 8
    half = tokens // 2
    ring = lanes // 2
    group = INNER // GROUPS
    group_heads = HEADS // GROUPS
    me_col = lax.axis_index("col")
    me_row = lax.axis_index("row")
    hi, z = me_col // ring, me_col % ring

    offsets = []
    for k in range(ring):
        m = (k + 1) // 2
        dz = (ring // 2 - m) if k % 2 else -(ring // 2 - m)
        offsets += [(1, dz), (0, dz)]
    offsets = [o for o in offsets if o != (0, 0)]
    col_peers = [((hi + dy) % 2) * ring + (z + dz + ring) % ring for dy, dz in offsets]
    row_peers = [(me_row + k) % tall for k in range(1, tall)]

    barrier = pltpu.get_barrier_semaphore()
    for p in col_peers:
        pl.semaphore_signal(barrier, inc=1, device_id={"col": p}, device_id_type=pl.DeviceIdType.MESH)
    for q in row_peers:
        pl.semaphore_signal(barrier, inc=1, device_id={"row": q}, device_id_type=pl.DeviceIdType.MESH)

    def send_col(src, dst, out_sem, in_sem, p):
        pltpu.make_async_remote_copy(
            src_ref=src, dst_ref=dst, send_sem=out_sem, recv_sem=in_sem,
            device_id={"col": p}, device_id_type=pl.DeviceIdType.MESH,
        ).start()

    def send_row(src, dst, out_sem, in_sem, q):
        pltpu.make_async_remote_copy(
            src_ref=src, dst_ref=dst, send_sem=out_sem, recv_sem=in_sem,
            device_id={"row": q}, device_id_type=pl.DeviceIdType.MESH,
        ).start()

    def wait_for(ref, sem):
        pltpu.make_async_copy(ref, ref, sem).wait()

    rows = lax.broadcasted_iota(jnp.int32, (tokens, tokens), 0)
    cols = lax.broadcasted_iota(jnp.int32, (tokens, tokens), 1)
    causal = rows >= cols
    same = causal & ((rows & 7) == (cols & 7))
    channel = lax.broadcasted_iota(jnp.int32, (HEADS, INNER), 1)
    head = lax.broadcasted_iota(jnp.int32, (HEADS, INNER), 0)
    spread = ((channel >= head * HEAD) & (channel < (head + 1) * HEAD)).astype(BF16)
    bias = table_ref[pl.ds(step_ref[0], 1), :]

    dt_own = dt_ref[...].astype(F32).reshape(tokens, 2 * HEADS)
    dt_col = softplus(dt_own[:, HEADS:] + bias[:, HEADS:])
    log_col = dt_col * (-LOG2E * rates_ref[1:2, :])
    run_col = dot_exact(same.astype(BF16), log_col)
    run3 = run_col.reshape(lanes, 8, HEADS)
    end_col = run3[lanes - 1]
    to_end = jnp.exp2(end_col[None] - run3).reshape(tokens, HEADS)
    x_all = x_ref[...].astype(F32).reshape(tokens, INNER)
    u_col = (expand(dt_col, spread) * x_all).astype(BF16)
    bc_own = bc_ref[...].astype(F32).reshape(tokens, 4 * STATE)
    b_col = bc_own[:, 2 * STATE : 3 * STATE].astype(BF16)
    c_col = bc_own[:, 3 * STATE :].astype(BF16)
    wide = 8 * STATE
    fan = (
        (lax.broadcasted_iota(jnp.int32, (STATE, wide), 1) & (STATE - 1))
        == lax.broadcasted_iota(jnp.int32, (STATE, wide), 0)
    ).astype(BF16)
    own_col = (lax.broadcasted_iota(jnp.int32, (tokens, wide), 1) // STATE) == (
        lax.broadcasted_iota(jnp.int32, (tokens, wide), 0) & 7
    )
    b_wide = jnp.where(own_col, dot(b_col, fan), 0.0)
    c_wide = jnp.where(own_col, dot(c_col, fan), 0.0).astype(BF16)
    u_end = (expand(to_end, spread) * u_col.astype(F32)).astype(BF16)
    states = dot(b_wide.T.astype(BF16), u_end)
    f_send[...] = states.astype(BF16).reshape(8, STATE, INNER)
    t_send[...] = jnp.concatenate([end_col, jnp.zeros((8, 128 - HEADS), F32)], axis=1)

    pl.semaphore_wait(barrier, lanes - 1 + tall - 1)

    for p in col_peers:
        send_col(bc_ref.at[p], got_bc.at[me_col], m_out, m_in.at[0], p)
        send_col(dt_ref.at[p], got_dt.at[me_col], m_out, m_in.at[1], p)
    for q in row_peers:
        send_row(f_send.at[q], got_f.at[me_row], f_out.at[0], f_in.at[0], q)
        send_row(t_send, got_t.at[me_row], f_out.at[1], f_in.at[1], q)
    for g in range(GROUPS):
        part = pl.ds(g * group, group)
        for p in col_peers:
            send_col(x_ref.at[p, :, part], got_x.at[me_col, :, part], x_out.at[g], x_in.at[g], p)
    got_bc[me_col] = bc_ref[me_col]
    got_dt[me_col] = dt_ref[me_col]
    got_x[me_col] = x_ref[me_col]
    got_f[me_row] = f_send[me_row]
    got_t[me_row] = t_send[...]

    def weights_of(run, run_t, scores, bar, h):
        top = jnp.exp2(run[:half, h : h + 1] - run_t[h : h + 1, :half] + bar[:half, :half]) * scores[:half, :half]
        low = jnp.exp2(run[half:, h : h + 1] - run_t[h : h + 1, :] + bar[half:, :]) * scores[half:, :]
        return top.astype(BF16), low.astype(BF16)

    def transposed(run):
        return jnp.concatenate([run, jnp.zeros((tokens, 128 - HEADS), F32)], axis=1).T

    def scores_of(c, b):
        return lax.dot_general(c, b, (((1,), (1,)), ((), ())), preferred_element_type=F32)

    lane = lax.broadcasted_iota(jnp.int32, (1, 128), 1)

    bar_col = jnp.where(same, 0.0, -1e30)
    scores_col = scores_of(c_col, b_col)
    run_col_t = transposed(run_col)
    skip_wide = expand(skip_ref[...], spread, 3)
    for pair in range(HEADS // 2):
        part = slice(pair * 128, pair * 128 + 128)
        top0, low0 = weights_of(run_col, run_col_t, scores_col, bar_col, 2 * pair)
        top1, low1 = weights_of(run_col, run_col_t, scores_col, bar_col, 2 * pair + 1)
        u = u_col[:, part]
        kept = skip_wide[:, part] * x_all[:, part]
        acc[:half, part] = jnp.where(lane < HEAD, dot(top0, u[:half]), dot(top1, u[:half])) + kept[:half]
        acc[half:, part] = jnp.where(lane < HEAD, dot(low0, u), dot(low1, u)) + kept[half:]

    wait_for(got_f.at[pl.ds(0, tall - 1)], f_in.at[0])
    wait_for(got_t.at[pl.ds(0, tall - 1)], f_in.at[1])
    ends = jnp.concatenate([got_t[k, pl.ds(me_row, 1), :] for k in range(tall)], axis=0)
    decay = expand(jnp.exp2(ends[:, :HEADS]), spread, 3)
    carry = jnp.zeros((STATE, INNER), F32)
    for k in range(tall):
        s_send[k] = carry.astype(BF16)
        if k < tall - 1:
            carry = decay[k : k + 1] * carry + got_f[k].astype(F32)

    wait_for(got_bc.at[pl.ds(0, lanes - 1)], m_in.at[0])
    wait_for(got_dt.at[pl.ds(0, lanes - 1)], m_in.at[1])
    for q in row_peers:
        send_row(s_send.at[q], got_s.at[me_row], s_out, s_in, q)
    got_s[me_row] = s_send[me_row]
    bc_line = got_bc[...].astype(F32).reshape(tokens, 4 * STATE)
    dt_line = got_dt[...].astype(F32).reshape(tokens, 2 * HEADS)
    dt_row = softplus(dt_line[:, :HEADS] + bias[:, :HEADS])
    run_row = dot_exact(causal.astype(BF16), dt_row * (-LOG2E * rates_ref[0:1, :]))
    run_row_t = transposed(run_row)
    scores_row = scores_of(bc_line[:, STATE : 2 * STATE].astype(BF16), bc_line[:, :STATE].astype(BF16))
    bar_row = jnp.where(causal, 0.0, -1e30)
    u_row_s[...] = expand(dt_row, spread)
    for h in range(HEADS):
        top, low = weights_of(run_row, run_row_t, scores_row, bar_row, h)
        w_row[h, :half, :half] = top
        w_row[h, half:, :] = low

    gate = gate_ref[...].astype(F32).reshape(tokens, INNER)
    act[...] = 0.5 * gate * (1.0 + jnp.tanh(0.5 * gate))

    wait_for(got_s.at[pl.ds(0, tall - 1)], s_in)
    entering = dot(c_wide, got_s[...].astype(F32).reshape(wide, INNER).astype(BF16))
    acc[...] += expand(jnp.exp2(run_col), spread) * entering

    for g in range(GROUPS):
        part = pl.ds(g * group, group)
        wait_for(got_x.at[pl.ds(0, lanes - 1), :, part], x_in.at[g])
        x_line = got_x[:, :, part].astype(F32).reshape(tokens, group)
        u = (u_row_s[:, part] * x_line).astype(BF16)
        for i in range(group_heads // 2):
            h = g * group_heads + 2 * i
            u_pair = u[:, i * 128 : i * 128 + 128]
            top = jnp.where(
                lane < HEAD, dot(w_row[h, :half, :half], u_pair[:half]), dot(w_row[h + 1, :half, :half], u_pair[:half])
            )
            low = jnp.where(lane < HEAD, dot(w_row[h, half:, :], u_pair), dot(w_row[h + 1, half:, :], u_pair))
            here = pl.ds(h * HEAD, 128)
            y_send[: lanes // 2, :, here] = top.reshape(lanes // 2, 8, 128).astype(BF16)
            y_send[lanes // 2 :, :, here] = low.reshape(lanes // 2, 8, 128).astype(BF16)
        for p in col_peers:
            send_col(y_send.at[p, :, part], got_y.at[me_col, :, part], y_out.at[g], y_in.at[g], p)
        got_y[me_col, :, part] = y_send[me_col, :, part]

    power = jnp.zeros((tokens, 128), F32)
    for g in range(GROUPS):
        part = pl.ds(g * group, group)
        wait_for(got_y.at[pl.ds(0, lanes - 1), :, part], y_in.at[g])
        y_row = got_y[:, :, part].astype(F32).reshape(tokens, group)
        v = (y_row + acc[:, part]) * act[:, part]
        mixed[:, part] = v
        for i in range(group // 128):
            w = v[:, i * 128 : i * 128 + 128]
            power += w * w
    scale = lax.rsqrt(jnp.sum(power, axis=1, keepdims=True) * (1.0 / INNER) + 1e-05)
    out_ref[...] = (mixed[...] * scale * gain_ref[...]).reshape(lanes, 8, INNER).astype(BF16)

    wait_for(bc_ref.at[pl.ds(0, lanes - 1)], m_out)
    wait_for(dt_ref.at[pl.ds(0, lanes - 1)], m_out)
    wait_for(f_send.at[pl.ds(0, tall - 1)], f_out.at[0])
    wait_for(got_t.at[pl.ds(0, tall - 1)], f_out.at[1])
    wait_for(s_send.at[pl.ds(0, tall - 1)], s_out)
    for g in range(GROUPS):
        part = pl.ds(g * group, group)
        wait_for(x_ref.at[pl.ds(0, lanes - 1), :, part], x_out.at[g])
        wait_for(y_send.at[pl.ds(0, lanes - 1), :, part], y_out.at[g])


def body(lanes, tall, x_in, gate_in, proj_bc, dt_raw, step_index, step_table, rates, skip, norm_gain):
    tokens = lanes * 8
    vmem = pl.BlockSpec(memory_space=pltpu.VMEM)
    smem = pl.BlockSpec(memory_space=pltpu.SMEM)
    dma = pltpu.SemaphoreType.DMA
    out = pl.pallas_call(
        functools.partial(kernel, lanes, tall),
        out_shape=jax.ShapeDtypeStruct((lanes, 8, INNER), BF16),
        in_specs=[smem] + [vmem] * 8,
        out_specs=vmem,
        scratch_shapes=[
            pltpu.VMEM((lanes, 8, INNER), BF16),
            pltpu.VMEM((lanes, 8, 4 * STATE), BF16),
            pltpu.VMEM((lanes, 8, 2 * HEADS), BF16),
            pltpu.VMEM((lanes, 8, INNER), BF16),
            pltpu.VMEM((lanes, 8, INNER), BF16),
            pltpu.VMEM((8, STATE, INNER), BF16),
            pltpu.VMEM((tall, STATE, INNER), BF16),
            pltpu.VMEM((8, 128), F32),
            pltpu.VMEM((tall, 8, 128), F32),
            pltpu.VMEM((tall, STATE, INNER), BF16),
            pltpu.VMEM((8, STATE, INNER), BF16),
            pltpu.VMEM((HEADS, tokens, tokens), BF16),
            pltpu.VMEM((tokens, INNER), F32),
            pltpu.VMEM((tokens, INNER), F32),
            pltpu.VMEM((tokens, INNER), F32),
            pltpu.VMEM((tokens, INNER), F32),
            dma((GROUPS,)),
            dma((GROUPS,)),
            dma,
            dma((2,)),
            dma((GROUPS,)),
            dma((GROUPS,)),
            dma((2,)),
            dma((2,)),
            dma,
            dma,
        ],
        compiler_params=pltpu.CompilerParams(
            collective_id=0, has_side_effects=True, vmem_limit_bytes=60 * 1024 * 1024
        ),
    )(
        step_index,
        step_table,
        rates,
        skip.reshape(1, HEADS),
        norm_gain.reshape(1, INNER),
        x_in.reshape(lanes, 8, INNER),
        gate_in.reshape(lanes, 8, INNER),
        proj_bc.reshape(lanes, 8, 4 * STATE),
        dt_raw.reshape(lanes, 8, 2 * HEADS),
    )
    return out.reshape(1, lanes, 8, INNER)


def solution(mesh):
    tile = P("img", "row", "col", None)
    return jax.shard_map(
        functools.partial(body, mesh.shape["col"], mesh.shape["row"]),
        mesh=mesh,
        in_specs=(tile, tile, tile, tile, P("img"), P(), P(), P(), P()),
        out_specs=tile,
        check_vma=False,
    )
```

time: 347 us -> 100 us (0.29); the launches traced: 343 us -> 100 us
  Pallas kernels: 0 us -> 94.8 us
  waiting for transfers between devices: 87.2 us -> 0 us
  blocking collectives: 59 us -> 0 us
  local copies, waits for them, and re-layouts: 59.5 us -> 4.61 us
  other arithmetic: 47.5 us -> 0 us
  matrix products: 45.8 us -> 0 us
  starting transfers between devices: 29.3 us -> 0 us
  between operations: 14.4 us -> 0.68 us
    pallas_call x0 -> x1, Pallas kernels: none -> 94.8 us  [body(): pl.pallas_call(functools.partial(kernel, lanes, tall), out_shape=jax.Shap...]
    all_gather x1 -> x0, waiting for transfers between devices: 54 us -> none  [prefix(): gathered = jax.tree.map(lambda a: lax.all_gather(a, axis), part)]
    dot_general x10 -> x0, matrix products: 45.8 us -> none  [the longest x2 12.6 us: segment_scan(): jnp.einsum('lkijh,lkjhp->lkihp', weights, values, precision=lax.Precision...]
    all_gather x1 -> x0, blocking collectives: 41.1 us -> none  [prefix(): gathered = jax.tree.map(lambda a: lax.all_gather(a, axis), part)]
    all_to_all x3 -> x0, waiting for transfers between devices: 33.1 us -> none  [the longest x1 18.3 us: body(): lax.all_to_all(sent_rows[0], 'col', split_axis=0, concat_axis=1, tiled=True)]
    all_to_all x3 -> x0, starting transfers between devices: 29.3 us -> none  [the longest x1 18.1 us: body(): lax.all_to_all(sent_rows[1], 'col', split_axis=0, concat_axis=1, tiled=True)]
    all_to_all x1 -> x0, blocking collectives: 17.9 us -> none  [body(): lax.all_to_all(sent_rows[2], 'col', split_axis=0, concat_axis=1, tiled=True)]
    convert_element_type x6 -> x0, local copies, waits for them, and re-layouts: 17.6 us -> none  [the longest x2 9.17 us: run_lines(): return outputs.astype(jnp.bfloat16).reshape(line_count, length, channels)]
  transfers between devices with their start and end apart: 4 -> 0, of which waited for: 3 -> 0; matrix products, arithmetic and copies ran while one was open for 29% -> 0% of each run, Pallas kernels for 0% -> 0%
where the time goes in v1:
time: 100 us
  Pallas kernels  94.8 us (95%)
  local copies, waits for them, and re-layouts  4.61 us (5%)
    pallas_call x1, Pallas kernels, body(): pl.pallas_call(functools.partial(kernel, lanes, tall), out_shape=jax.Shap...  94.8 us
    unnamed x4, local copies, waits for them, and re-layouts  4.01 us

profile of v1, /device:TPU:6, one launch (start us, length us, event | category | flops | bytes accessed | tf_op | source)
XLA Modules:
  0.0 100.1 jit_solution(940184492706099247)
XLA Ops:
  0.0 0.0 copy-start
  0.7 0.0 copy-done
  0.7 0.6 reshape.22.gain_ref
  1.3 1.9 %copy.10.table_ref = f32[1000,48]{1,0:T(8,128)} copy(f32[1000,48]{0,1:T(8,128)} %param.14) | data formatting | bytes 384000 | tf_op args[5]
  3.2 94.8 %shard_map.91 = bf16[32,8,1536]{2,1,0:T(8,128)(2,1)} custom-call(s32[1]{0:T(128)S(6)} %copy.12.step_ref, f32[1000,48]{1,0:T(8,128)} %copy.10.table_ref, f32[2,24]{1,0:T(2,128)} %rates_ref.1, f32[1,24]{1,0:T(1,128)} %bitcast.11, f32[1,1536]{1,0:T(1,128)} %reshape.22.gain_ref, bf16[32,8,1536]{2,1,0:T(8,128)(2,1)} %bitcast.7, bf16[32,8,1536]{2,1,0:T(8,128)(2,1)} %bitcast.8, ...), custom_call_target="tpu_custom_call" | custom-call | tf_op jit(solution)/shard_map/pallas_call | solution.py:252
  98.0 2.1 %copy.13 = bf16[1,32,8,1536]{3,2,1,0:T(8,128)(2,1)} copy(bf16[1,32,8,1536]{3,2,1,0:T(8,128)(2,1)} %bitcast.6) | data formatting | bytes 1572864
Async XLA Ops:
  0.0 0.7 copy-start

commit v2 on v1

v2 whole, which is shorter than its diff:
```python
import functools

import jax
import jax.numpy as jnp
from jax import lax
from jax.experimental import pallas as pl
from jax.experimental.pallas import tpu as pltpu
from jax.sharding import PartitionSpec as P

HEADS = 24
HEAD = 64
STATE = 16
INNER = HEADS * HEAD
GROUPS = 4
WINDOW = 8
AHEAD = 2
LOG2E = 1.4426950408889634
F32 = jnp.float32
BF16 = jnp.bfloat16


def dot(a, b):
    return jnp.dot(a, b, preferred_element_type=F32)


def split(v, pieces):
    parts = []
    for _ in range(pieces):
        part = v.astype(BF16)
        parts.append(part)
        v = v - part.astype(F32)
    return parts


def dot_exact(zero_one, v, pieces=3):
    return sum(dot(zero_one, part) for part in split(v, pieces))


def expand(v, heads_to_channels, pieces=2):
    return sum(dot(part, heads_to_channels) for part in split(v, pieces))


def softplus(v):
    return jnp.maximum(v, 0.0) + jnp.log(1.0 + jnp.exp(-jnp.abs(v)))


def kernel(
    lanes, tall, step_ref, table_hbm, rates_ref, skip_ref, gain_ref, x_hbm, gate_hbm, bc_hbm, dt_hbm, out_ref,
    table_ref, x_ref, gate_ref, bc_ref, dt_ref, load_sem,
    got_x, got_bc, got_dt, y_send, got_y, f_send, got_f, t_send, got_t, s_send, got_s,
    l_send, got_l, i_send, got_i, e_send, got_e, w_row, u_row_s, end_s, near, acc, act, mixed,
    x_out, x_in, m_out, m_in, y_out, y_in, f_out, f_in, s_out, s_in, l_out, l_in, i_out, i_in, e_out, e_in,
):
    tile_rows = x_ref.shape[0]
    tokens = tile_rows * 8
    half = tokens // 2
    windows = lanes // WINDOW
    lines = tile_rows // WINDOW
    group = INNER // GROUPS
    group_heads = HEADS // GROUPS
    middle = WINDOW // 2
    me_col = lax.axis_index("col")
    me_row = lax.axis_index("row")

    def around(c):
        return (c + 2 * lanes) % lanes

    def rows_of(c):
        return pl.ds(((c + middle) % WINDOW) * lines, lines)

    order = sorted(range(1, middle + 1), reverse=True)
    to = [d for k in order for d in ((k, -k) if k < middle else (k,))]
    fro = [d for k in order for d in ((-k, k) if k < middle else (-k,))]
    row_peers = [(me_row + k) % tall for k in range(1, tall)]
    after, before, across = around(me_col + WINDOW), around(me_col - WINDOW), around(me_col + 2 * WINDOW)
    place = ((me_col + middle - 1) % lanes) // WINDOW
    cut = around(middle - me_col)
    cut_in = jnp.where(place == 0, cut, WINDOW)
    cut_out = jnp.where(place == 0, cut, 0)

    barrier = pltpu.get_barrier_semaphore()

    def greet(**device):
        pl.semaphore_signal(barrier, inc=1, device_id=device, device_id_type=pl.DeviceIdType.MESH)

    near_set = sorted(set(to) | set(fro))
    for d in near_set:
        greet(col=around(me_col + d))
    for c in (after, before, across):
        greet(col=c)
    for q in row_peers:
        greet(row=q)

    loads = []
    for i, (src, dst) in enumerate(
        ((bc_hbm, bc_ref), (dt_hbm, dt_ref), (table_hbm, table_ref), (x_hbm, x_ref), (gate_hbm, gate_ref))
    ):
        loads.append(pltpu.make_async_copy(src, dst, load_sem.at[i]))
        loads[-1].start()

    def send_col(src, dst, out_sem, in_sem, p):
        pltpu.make_async_remote_copy(
            src_ref=src, dst_ref=dst, send_sem=out_sem, recv_sem=in_sem,
            device_id={"col": p}, device_id_type=pl.DeviceIdType.MESH,
        ).start()

    def send_row(src, dst, out_sem, in_sem, q):
        pltpu.make_async_remote_copy(
            src_ref=src, dst_ref=dst, send_sem=out_sem, recv_sem=in_sem,
            device_id={"row": q}, device_id_type=pl.DeviceIdType.MESH,
        ).start()

    def wait_for(ref, sem):
        pltpu.make_async_copy(ref, ref, sem).wait()

    rows = lax.broadcasted_iota(jnp.int32, (tokens, tokens), 0)
    cols = lax.broadcasted_iota(jnp.int32, (tokens, tokens), 1)
    causal = rows >= cols
    same = causal & ((rows & 7) == (cols & 7))
    channel = lax.broadcasted_iota(jnp.int32, (HEADS, INNER), 1)
    head = lax.broadcasted_iota(jnp.int32, (HEADS, INNER), 0)
    spread = ((channel >= head * HEAD) & (channel < (head + 1) * HEAD)).astype(BF16)

    def widen(v, kept, count):
        wide = count * STATE
        fan = (
            (lax.broadcasted_iota(jnp.int32, (STATE, wide), 1) & (STATE - 1))
            == lax.broadcasted_iota(jnp.int32, (STATE, wide), 0)
        ).astype(BF16)
        return jnp.where(kept, dot(v, fan), 0.0)

    for i in range(4):
        loads[i].wait()
    chosen = (lax.broadcasted_iota(jnp.int32, (8, table_ref.shape[1]), 1) == step_ref[0]).astype(BF16)
    bias = sum(
        lax.dot_general(chosen, part, (((1,), (1,)), ((), ())), preferred_element_type=F32)
        for part in split(table_ref[...], 3)
    )[0:1]
    dt_own = dt_ref[...].astype(F32).reshape(tokens, 2 * HEADS)
    dt_col = softplus(dt_own[:, HEADS:] + bias[:, HEADS:])
    log_col = dt_col * (-LOG2E * rates_ref[1:2, :])
    run_col = dot_exact(same.astype(BF16), log_col)
    run3 = run_col.reshape(tile_rows, 8, HEADS)
    end_col = run3[tile_rows - 1]
    to_end = jnp.exp2(end_col[None] - run3).reshape(tokens, HEADS)
    x_all = x_ref[...].astype(F32).reshape(tokens, INNER)
    u_col = (expand(dt_col, spread) * x_all).astype(BF16)
    bc_own = bc_ref[...].astype(F32).reshape(tokens, 4 * STATE)
    b_col = bc_own[:, 2 * STATE : 3 * STATE].astype(BF16)
    c_col = bc_own[:, 3 * STATE :].astype(BF16)
    own_col = (lax.broadcasted_iota(jnp.int32, (tokens, 8 * STATE), 1) // STATE) == (
        lax.broadcasted_iota(jnp.int32, (tokens, 8 * STATE), 0) & 7
    )
    c_wide = widen(c_col, own_col, 8).astype(BF16)
    u_end = (expand(to_end, spread) * u_col.astype(F32)).astype(BF16)
    states = dot(widen(b_col, own_col, 8).T.astype(BF16), u_end)
    f_send[...] = states.astype(BF16).reshape(8, STATE, INNER)
    t_send[...] = jnp.concatenate([end_col, jnp.zeros((8, 128 - HEADS), F32)], axis=1)

    def send_tokens(g):
        part = pl.ds(g * group, group)
        for d in to:
            c = around(me_col + d)
            send_col(x_ref.at[rows_of(c), :, part], got_x.at[middle - d, :, :, part], x_out.at[g], x_in.at[g], c)

    pl.semaphore_wait(barrier, len(near_set) + 3 + tall - 1)

    for d in to:
        c = around(me_col + d)
        send_col(bc_ref.at[rows_of(c)], got_bc.at[middle - d], m_out.at[0], m_in.at[0], c)
        send_col(dt_ref.at[rows_of(c)], got_dt.at[middle - d], m_out.at[1], m_in.at[1], c)
    for g in range(AHEAD):
        send_tokens(g)
    for q in row_peers:
        send_row(f_send.at[q], got_f.at[me_row], f_out.at[0], f_in.at[0], q)
        send_row(t_send, got_t.at[me_row], f_out.at[1], f_in.at[1], q)
    got_bc[middle] = bc_ref[rows_of(me_col)]
    got_dt[middle] = dt_ref[rows_of(me_col)]
    got_x[middle] = x_ref[rows_of(me_col)]
    got_f[me_row] = f_send[me_row]
    got_t[me_row] = t_send[...]

    def wait_near(ref, sem):
        wait_for(ref.at[pl.ds(0, WINDOW - 1)], sem)

    def weights_of(run, run_t, scores, bar, h):
        top = jnp.exp2(run[:half, h : h + 1] - run_t[h : h + 1, :half] + bar[:half, :half]) * scores[:half, :half]
        low = jnp.exp2(run[half:, h : h + 1] - run_t[h : h + 1, :] + bar[half:, :]) * scores[half:, :]
        return top.astype(BF16), low.astype(BF16)

    def transposed(run):
        return jnp.concatenate([run, jnp.zeros((tokens, 128 - HEADS), F32)], axis=1).T

    def scores_of(c, b):
        return lax.dot_general(c, b, (((1,), (1,)), ((), ())), preferred_element_type=F32)

    lane = lax.broadcasted_iota(jnp.int32, (1, 128), 1)

    wait_near(got_bc, m_in.at[0])
    wait_near(got_dt, m_in.at[1])
    line_size = 8 * lines
    tile_i, tile_j = rows // line_size, cols // line_size
    line_i, line_j = (rows // 8) % lines, (cols // 8) % lines
    joined = causal & (line_i == line_j) & ((tile_i >= cut_out) == (tile_j >= cut_out))
    bc_line = got_bc[...].astype(F32).reshape(tokens, 4 * STATE)
    dt_line = got_dt[...].astype(F32).reshape(tokens, 2 * HEADS)
    dt_row = softplus(dt_line[:, :HEADS] + bias[:, :HEADS])
    log_row = dt_row * (-LOG2E * rates_ref[0:1, :])
    run_row = dot_exact(joined.astype(BF16), log_row)
    ends_row = run_row.reshape(WINDOW, lines, 8, HEADS)[WINDOW - 1, :, 7:8, :]
    run4 = run_row.reshape(WINDOW, lines, 8, HEADS)
    tile4 = lax.broadcasted_iota(jnp.int32, (WINDOW, lines, 8, HEADS), 0)
    to_end_row = jnp.where(tile4 >= cut_out, jnp.exp2(ends_row[None] - run4), 0.0).reshape(tokens, HEADS)
    from_start = jnp.where(tile4 < cut_in, jnp.exp2(run4), 0.0).reshape(tokens, HEADS)
    own_line = (lax.broadcasted_iota(jnp.int32, (tokens, lines * STATE), 1) // STATE) == (
        lax.broadcasted_iota(jnp.int32, (tokens, lines * STATE), 0) // 8
    ) % lines
    b_row = bc_line[:, :STATE].astype(BF16)
    c_row = bc_line[:, STATE : 2 * STATE].astype(BF16)
    b_lines = widen(b_row, own_line, lines).T.astype(BF16)
    c_lines = widen(c_row, own_line, lines).astype(BF16)
    u_row_s[...] = expand(dt_row, spread)
    end_s[...] = expand(to_end_row, spread)
    line_decay = jnp.exp2(ends_row.reshape(lines, HEADS))
    e_send[...] = jnp.concatenate(
        [
            jnp.concatenate([line_decay, jnp.zeros((8 - lines, HEADS), F32)], axis=0),
            jnp.zeros((8, 128 - HEADS), F32),
        ],
        axis=1,
    )
    own_decay = expand(line_decay, spread, 3)
    send_col(e_send, got_e, e_out, e_in, after)
    scores_row = scores_of(c_row, b_row)
    run_row_t = transposed(run_row)
    bar_row = jnp.where(joined, 0.0, -1e30)
    for h in range(HEADS):
        top, low = weights_of(run_row, run_row_t, scores_row, bar_row, h)
        w_row[h, :half, :half] = top
        w_row[h, half:, :] = low

    def enter(g):
        part = pl.ds(g * group, group)
        wait_near(got_x.at[:, :, :, part], x_in.at[g])
        x_line = got_x[:, :, :, part].astype(F32).reshape(tokens, group)
        u = (u_row_s[:, part] * x_line).astype(BF16)
        u_end = (end_s[:, part] * u.astype(F32)).astype(BF16)
        state = dot(b_lines, u_end)
        l_send[:, :, part] = state.reshape(lines, STATE, group).astype(BF16)
        send_col(l_send.at[:, :, part], got_l.at[:, :, part], l_out.at[g], l_in.at[g], after)

        @pl.when((place == 0) | (place == windows - 1))
        def _():
            i_send[:, :, part] = state.reshape(lines, STATE, group).astype(BF16)
            pass_on(g)

        if g + AHEAD < GROUPS:
            send_tokens(g + AHEAD)
        for i in range(group_heads // 2):
            h = g * group_heads + 2 * i
            u_pair = u[:, i * 128 : i * 128 + 128]
            here = pl.ds(h * HEAD, 128)
            near[:half, here] = jnp.where(
                lane < HEAD, dot(w_row[h, :half, :half], u_pair[:half]), dot(w_row[h + 1, :half, :half], u_pair[:half])
            )
            near[half:, here] = jnp.where(
                lane < HEAD, dot(w_row[h, half:, :], u_pair), dot(w_row[h + 1, half:, :], u_pair)
            )

    def pass_on(g):
        part = pl.ds(g * group, group)
        send_col(i_send.at[:, :, part], got_i.at[:, :, part], i_out.at[g], i_in.at[g], across)

    def lined(v, g):
        return v[:, g * group : (g + 1) * group].reshape(lines, 1, group)

    def second(g):
        part = pl.ds(g * group, group)
        wait_for(got_l.at[:, :, part], l_in.at[g])

        @pl.when(place == 1)
        def _():
            joint = lined(own_decay, g) * got_l[:, :, part].astype(F32) + l_send[:, :, part].astype(F32)
            i_send[:, :, part] = joint.astype(BF16)
            pass_on(g)

    def finish(g, before_decay):
        part = pl.ds(g * group, group)
        wait_for(got_i.at[:, :, part], i_in.at[g])
        earlier = jnp.where(place == 1, 0.0, got_i[:, :, part].astype(F32))
        entering = lined(before_decay, g) * earlier + got_l[:, :, part].astype(F32)

        @pl.when(place == 2)
        def _():
            joint = lined(own_decay, g) * entering + l_send[:, :, part].astype(F32)
            i_send[:, :, part] = joint.astype(BF16)
            pass_on(g)

        carried = dot(c_lines, entering.reshape(lines * STATE, group).astype(BF16))
        y = near[:, part] + expand(from_start, spread[:, g * group : (g + 1) * group]) * carried
        y_send[:, :, :, part] = y.reshape(WINDOW, lines, 8, group).astype(BF16)
        for d in fro:
            send_col(
                y_send.at[middle + d, :, :, part], got_y.at[rows_of(me_col), :, part], y_out.at[g], y_in.at[g],
                around(me_col + d),
            )
        got_y[rows_of(me_col), :, part] = y_send[middle, :, :, part]

    for g in range(min(2, GROUPS)):
        enter(g)

    wait_for(got_f.at[pl.ds(0, tall - 1)], f_in.at[0])
    wait_for(got_t.at[pl.ds(0, tall - 1)], f_in.at[1])
    ends = jnp.concatenate([got_t[k, pl.ds(me_row, 1), :] for k in range(tall)], axis=0)
    decay = expand(jnp.exp2(ends[:, :HEADS]), spread, 3)
    carry = jnp.zeros((STATE, INNER), F32)
    for k in range(tall):
        s_send[k] = carry.astype(BF16)
        if k < tall - 1:
            carry = decay[k : k + 1] * carry + got_f[k].astype(F32)
    for q in row_peers:
        send_row(s_send.at[q], got_s.at[me_row], s_out, s_in, q)
    got_s[me_row] = s_send[me_row]

    def column_local():
        bar_col = jnp.where(same, 0.0, -1e30)
        scores_col = scores_of(c_col, b_col)
        run_col_t = transposed(run_col)
        skip_wide = expand(skip_ref[...], spread, 3)
        for pair in range(HEADS // 2):
            part = slice(pair * 128, pair * 128 + 128)
            top0, low0 = weights_of(run_col, run_col_t, scores_col, bar_col, 2 * pair)
            top1, low1 = weights_of(run_col, run_col_t, scores_col, bar_col, 2 * pair + 1)
            u = u_col[:, part]
            kept = skip_wide[:, part] * x_all[:, part]
            acc[:half, part] = jnp.where(lane < HEAD, dot(top0, u[:half]), dot(top1, u[:half])) + kept[:half]
            acc[half:, part] = jnp.where(lane < HEAD, dot(low0, u), dot(low1, u)) + kept[half:]

    for g in range(2, GROUPS):
        enter(g)
        if g == 2:
            column_local()
    if GROUPS <= 2:
        column_local()

    wait_for(got_e, e_in)
    before_decay = expand(got_e[:lines, :HEADS], spread, 3)
    second(0)
    for g in range(GROUPS):
        if g + 1 < GROUPS:
            second(g + 1)
        finish(g, before_decay)

    loads[4].wait()
    gate = gate_ref[...].astype(F32).reshape(tokens, INNER)
    act[...] = 0.5 * gate * (1.0 + jnp.tanh(0.5 * gate))

    wait_for(got_s.at[pl.ds(0, tall - 1)], s_in)
    entering_col = dot(c_wide, got_s[...].astype(F32).reshape(8 * STATE, INNER).astype(BF16))
    acc[...] += expand(jnp.exp2(run_col), spread) * entering_col

    power = jnp.zeros((tokens, 128), F32)
    for g in range(GROUPS):
        part = pl.ds(g * group, group)
        wait_for(got_y.at[pl.ds(0, (WINDOW - 1) * lines), :, part], y_in.at[g])
        y_row = got_y[:, :, part].astype(F32).reshape(tokens, group)
        v = (y_row + acc[:, part]) * act[:, part]
        mixed[:, part] = v
        for i in range(group // 128):
            w = v[:, i * 128 : i * 128 + 128]
            power += w * w
    scale = lax.rsqrt(jnp.sum(power, axis=1, keepdims=True) * (1.0 / INNER) + 1e-05)
    for i in range(INNER // 128):
        here = pl.ds(i * 128, 128)
        out_ref[:, :, here] = (mixed[:, here] * scale * gain_ref[i : i + 1, :]).reshape(tile_rows, 8, 128).astype(BF16)

    wait_near(got_bc, m_out.at[0])
    wait_near(got_dt, m_out.at[1])
    wait_for(f_send.at[pl.ds(0, tall - 1)], f_out.at[0])
    wait_for(got_t.at[pl.ds(0, tall - 1)], f_out.at[1])
    wait_for(s_send.at[pl.ds(0, tall - 1)], s_out)
    wait_for(e_send, e_out)
    for g in range(GROUPS):
        part = pl.ds(g * group, group)
        wait_near(got_x.at[:, :, :, part], x_out.at[g])
        wait_near(y_send.at[:, :, :, part], y_out.at[g])
        wait_for(l_send.at[:, :, part], l_out.at[g])
        wait_for(i_send.at[:, :, part], i_out.at[g])


def body(lanes, tall, x_in, gate_in, proj_bc, dt_raw, step_index, step_table, rates, skip, norm_gain):
    _, tile_rows, tile_cols, _ = x_in.shape
    tokens = tile_rows * tile_cols
    lines = tile_rows // WINDOW
    steps = step_table.shape[0]
    vmem = pl.BlockSpec(memory_space=pltpu.VMEM)
    smem = pl.BlockSpec(memory_space=pltpu.SMEM)
    hbm = pl.BlockSpec(memory_space=pl.ANY)
    dma = pltpu.SemaphoreType.DMA
    out = pl.pallas_call(
        functools.partial(kernel, lanes, tall),
        out_shape=jax.ShapeDtypeStruct((tile_rows, 8, INNER), BF16),
        in_specs=[smem, hbm, vmem, vmem, vmem, hbm, hbm, hbm, hbm],
        out_specs=vmem,
        scratch_shapes=[
            pltpu.VMEM((2 * HEADS, steps), F32),
            pltpu.VMEM((tile_rows, 8, INNER), BF16),
            pltpu.VMEM((tile_rows, 8, INNER), BF16),
            pltpu.VMEM((tile_rows, 8, 4 * STATE), BF16),
            pltpu.VMEM((tile_rows, 8, 2 * HEADS), BF16),
            dma((5,)),
            pltpu.VMEM((WINDOW, lines, 8, INNER), BF16),
            pltpu.VMEM((WINDOW, lines, 8, 4 * STATE), BF16),
            pltpu.VMEM((WINDOW, lines, 8, 2 * HEADS), BF16),
            pltpu.VMEM((WINDOW, lines, 8, INNER), BF16),
            pltpu.VMEM((tile_rows, 8, INNER), BF16),
            pltpu.VMEM((8, STATE, INNER), BF16),
            pltpu.VMEM((tall, STATE, INNER), BF16),
            pltpu.VMEM((8, 128), F32),
            pltpu.VMEM((tall, 8, 128), F32),
            pltpu.VMEM((tall, STATE, INNER), BF16),
            pltpu.VMEM((8, STATE, INNER), BF16),
            pltpu.VMEM((lines, STATE, INNER), BF16),
            pltpu.VMEM((lines, STATE, INNER), BF16),
            pltpu.VMEM((lines, STATE, INNER), BF16),
            pltpu.VMEM((lines, STATE, INNER), BF16),
            pltpu.VMEM((8, 128), F32),
            pltpu.VMEM((8, 128), F32),
            pltpu.VMEM((HEADS, tokens, tokens), BF16),
            pltpu.VMEM((tokens, INNER), F32),
            pltpu.VMEM((tokens, INNER), F32),
            pltpu.VMEM((tokens, INNER), F32),
            pltpu.VMEM((tokens, INNER), F32),
            pltpu.VMEM((tokens, INNER), F32),
            pltpu.VMEM((tokens, INNER), F32),
            dma((GROUPS,)),
            dma((GROUPS,)),
            dma((2,)),
            dma((2,)),
            dma((GROUPS,)),
            dma((GROUPS,)),
            dma((2,)),
            dma((2,)),
            dma,
            dma,
            dma((GROUPS,)),
            dma((GROUPS,)),
            dma((GROUPS,)),
            dma((GROUPS,)),
            dma,
            dma,
        ],
        compiler_params=pltpu.CompilerParams(
            collective_id=0, has_side_effects=True, vmem_limit_bytes=60 * 1024 * 1024
        ),
    )(
        step_index,
        step_table.T,
        rates,
        skip.reshape(1, HEADS),
        norm_gain.reshape(INNER // 128, 128),
        x_in.reshape(tile_rows, 8, INNER),
        gate_in.reshape(tile_rows, 8, INNER),
        proj_bc.reshape(tile_rows, 8, 4 * STATE),
        dt_raw.reshape(tile_rows, 8, 2 * HEADS),
    )
    return out.reshape(x_in.shape)


def solution(mesh):
    tile = P("img", "row", "col", None)
    return jax.shard_map(
        functools.partial(body, mesh.shape["col"], mesh.shape["row"]),
        mesh=mesh,
        in_specs=(tile, tile, tile, tile, P("img"), P(), P(), P(), P()),
        out_specs=tile,
        check_vma=False,
    )
```

time: 100 us -> 86.1 us (0.86)
  Pallas kernels: 94.8 us -> 82.8 us
  local copies, waits for them, and re-layouts: 4.61 us -> 2.06 us
    pallas_call x1, Pallas kernels: 94.8 us -> 82.8 us  [body(): pl.pallas_call(functools.partial(kernel, lanes, tall), out_shape=jax.Shap...]
    unnamed x4 -> x1, local copies, waits for them, and re-layouts: 4.01 us -> 2.06 us
where the time goes in v2:
time: 86.1 us; the launch traced here: 85.5 us
  Pallas kernels  82.8 us (96%)
  local copies, waits for them, and re-layouts  2.06 us (2%)
    pallas_call x1, Pallas kernels, body(): pl.pallas_call(functools.partial(kernel, lanes, tall), out_shape=jax.Shap...  82.8 us
    unnamed x1, local copies, waits for them, and re-layouts  2.06 us

profile of v2, /device:TPU:6, one launch (start us, length us, event | category | flops | bytes accessed | tf_op | source)
XLA Modules:
  0.0 85.5 jit_solution(6077111352230038728)
XLA Ops:
  0.7 82.8 %shard_map.91 = bf16[32,8,1536]{2,1,0:T(8,128)(2,1)} custom-call(s32[1]{0:T(128)S(6)} %copy.11.step_ref, f32[48,1000]{1,0:T(8,128)} %bitcast.11, f32[2,24]{1,0:T(2,128)} %rates_ref.1, f32[1,24]{1,0:T(1,128)} %bitcast.15, f32[12,128]{1,0:T(8,128)} %bitcast.14, bf16[32,8,1536]{2,1,0:T(8,128)(2,1)} %bitcast.9, bf16[32,8,1536]{2,1,0:T(8,128)(2,1)} %bitcast.10, ...), custom_call_target="tpu_custom_call" | custom-call | tf_op jit(solution)/shard_map/pallas_call | solution.py:400
  83.5 2.1 %copy.12 = bf16[1,32,8,1536]{3,2,1,0:T(8,128)(2,1)} copy(bf16[1,32,8,1536]{3,2,1,0:T(8,128)(2,1)} %bitcast.8) | data formatting | bytes 1572864

commit v3 on v2

--- a/solution.py
+++ b/solution.py
@@ -13,7 +13,7 @@
 INNER = HEADS * HEAD
 GROUPS = 4
 WINDOW = 8
-AHEAD = 2
+STAGES = 3
 LOG2E = 1.4426950408889634
 F32 = jnp.float32
 BF16 = jnp.bfloat16
@@ -49,7 +49,7 @@
     table_ref, x_ref, gate_ref, bc_ref, dt_ref, load_sem,
     got_x, got_bc, got_dt, y_send, got_y, f_send, got_f, t_send, got_t, s_send, got_s,
     l_send, got_l, i_send, got_i, e_send, got_e, w_row, u_row_s, end_s, near, acc, act, mixed,
-    x_out, x_in, m_out, m_in, y_out, y_in, f_out, f_in, s_out, s_in, l_out, l_in, i_out, i_in, e_out, e_in,
+    x_out, x_in, m_out, m_in, y_out, y_in, f_out, f_in, s_out, s_in, l_out, l_in, i_out, i_in, e_out, e_in, known,
 ):
     tile_rows = x_ref.shape[0]
     tokens = tile_rows * 8
@@ -83,10 +83,8 @@
     def greet(**device):
         pl.semaphore_signal(barrier, inc=1, device_id=device, device_id_type=pl.DeviceIdType.MESH)
 
-    near_set = sorted(set(to) | set(fro))
-    for d in near_set:
-        greet(col=around(me_col + d))
-    for c in (after, before, across):
+    greeted = [around(me_col + 1), around(me_col - 1)] + ([across] if windows > 2 else [])
+    for c in greeted:
         greet(col=c)
     for q in row_peers:
         greet(row=q)
@@ -157,23 +155,38 @@
     f_send[...] = states.astype(BF16).reshape(8, STATE, INNER)
     t_send[...] = jnp.concatenate([end_col, jnp.zeros((8, 128 - HEADS), F32)], axis=1)
 
-    def send_tokens(g):
-        part = pl.ds(g * group, group)
-        for d in to:
+    def send_states():
+        for q in row_peers:
+            send_row(f_send.at[q], got_f.at[me_row], f_out.at[0], f_in.at[0], q)
+            send_row(t_send, got_t.at[me_row], f_out.at[1], f_in.at[1], q)
+
+    def send_small(stage, d):
+        c = around(me_col + d)
+        send_col(bc_ref.at[rows_of(c)], got_bc.at[middle - d], m_out.at[0], m_in.at[2 * stage], c)
+        send_col(dt_ref.at[rows_of(c)], got_dt.at[middle - d], m_out.at[1], m_in.at[2 * stage + 1], c)
+
+    def send_tokens(g, chosen):
+        part = pl.ds(g * group, group)
+        for d in chosen:
             c = around(me_col + d)
             send_col(x_ref.at[rows_of(c), :, part], got_x.at[middle - d, :, :, part], x_out.at[g], x_in.at[g], c)
 
-    pl.semaphore_wait(barrier, len(near_set) + 3 + tall - 1)
-
-    for d in to:
-        c = around(me_col + d)
-        send_col(bc_ref.at[rows_of(c)], got_bc.at[middle - d], m_out.at[0], m_in.at[0], c)
-        send_col(dt_ref.at[rows_of(c)], got_dt.at[middle - d], m_out.at[1], m_in.at[1], c)
-    for g in range(AHEAD):
-        send_tokens(g)
-    for q in row_peers:
-        send_row(f_send.at[q], got_f.at[me_row], f_out.at[0], f_in.at[0], q)
-        send_row(t_send, got_t.at[me_row], f_out.at[1], f_in.at[1], q)
+    pl.semaphore_wait(barrier, len(greeted) + tall - 1)
+
+    reach = [0] + [1 << i for i in range(STAGES - 1)] + [middle]
+    for stage in range(STAGES):
+        if stage:
+            count = sum(reach[stage - 1] < abs(d) <= reach[stage] for d in fro)
+            wait_for(got_bc.at[pl.ds(0, count)], m_in.at[2 * stage - 2])
+            wait_for(got_dt.at[pl.ds(0, count)], m_in.at[2 * stage - 1])
+        chosen_to = [d for d in to if reach[stage] < abs(d) <= reach[stage + 1]]
+        for d in chosen_to:
+            send_small(stage, d)
+        for g in range(GROUPS):
+            send_tokens(g, chosen_to)
+        if stage == 0:
+            send_states()
+    pl.semaphore_signal(known, inc=1, device_id={"col": around(me_col - middle)}, device_id_type=pl.DeviceIdType.MESH)
     got_bc[middle] = bc_ref[rows_of(me_col)]
     got_dt[middle] = dt_ref[rows_of(me_col)]
     got_x[middle] = x_ref[rows_of(me_col)]
@@ -196,8 +209,10 @@
 
     lane = lax.broadcasted_iota(jnp.int32, (1, 128), 1)
 
-    wait_near(got_bc, m_in.at[0])
-    wait_near(got_dt, m_in.at[1])
+    last = sum(abs(d) > reach[STAGES - 1] for d in fro)
+    wait_for(got_bc.at[pl.ds(0, last)], m_in.at[2 * STAGES - 2])
+    wait_for(got_dt.at[pl.ds(0, last)], m_in.at[2 * STAGES - 1])
+    pl.semaphore_wait(known, 1)
     line_size = 8 * lines
     tile_i, tile_j = rows // line_size, cols // line_size
     line_i, line_j = (rows // 8) % lines, (cols // 8) % lines
@@ -254,8 +269,6 @@
             i_send[:, :, part] = state.reshape(lines, STATE, group).astype(BF16)
             pass_on(g)
 
-        if g + AHEAD < GROUPS:
-            send_tokens(g + AHEAD)
         for i in range(group_heads // 2):
             h = g * group_heads + 2 * i
             u_pair = u[:, i * 128 : i * 128 + 128]
@@ -436,7 +449,7 @@
             dma((GROUPS,)),
             dma((GROUPS,)),
             dma((2,)),
-            dma((2,)),
+            dma((2 * STAGES,)),
             dma((GROUPS,)),
             dma((GROUPS,)),
             dma((2,)),
@@ -449,6 +462,7 @@
             dma((GROUPS,)),
             dma,
             dma,
+            pltpu.SemaphoreType.REGULAR,
         ],
         compiler_params=pltpu.CompilerParams(
             collective_id=0, has_side_effects=True, vmem_limit_bytes=60 * 1024 * 1024

time: 86.1 us -> 84.7 us (0.984)
  the two profiles are of different devices: /device:TPU:6 before, /device:TPU:14 now
where the time goes in v3:
time: 84.7 us; the launch traced here: 84.5 us
  Pallas kernels  81.7 us (96%)
  local copies, waits for them, and re-layouts  2.06 us (2%)
    pallas_call x1, Pallas kernels, body(): pl.pallas_call(functools.partial(kernel, lanes, tall), out_shape=jax.Shap...  81.7 us
    unnamed x1, local copies, waits for them, and re-layouts  2.06 us

profile of v3, /device:TPU:14, one launch (start us, length us, event | category | flops | bytes accessed | tf_op | source)
XLA Modules:
  0.0 84.5 jit_solution(10691264038889888904)
XLA Ops:
  0.7 81.7 %shard_map.91 = bf16[32,8,1536]{2,1,0:T(8,128)(2,1)} custom-call(s32[1]{0:T(128)S(6)} %copy.11.step_ref, f32[48,1000]{1,0:T(8,128)} %bitcast.11, f32[2,24]{1,0:T(2,128)} %rates_ref.1, f32[1,24]{1,0:T(1,128)} %bitcast.15, f32[12,128]{1,0:T(8,128)} %bitcast.14, bf16[32,8,1536]{2,1,0:T(8,128)(2,1)} %bitcast.9, bf16[32,8,1536]{2,1,0:T(8,128)(2,1)} %bitcast.10, ...), custom_call_target="tpu_custom_call" | custom-call | tf_op jit(solution)/shard_map/pallas_call | solution.py:413
  82.4 2.1 %copy.12 = bf16[1,32,8,1536]{3,2,1,0:T(8,128)(2,1)} copy(bf16[1,32,8,1536]{3,2,1,0:T(8,128)(2,1)} %bitcast.8) | data formatting | bytes 1572864

commit v4 on v2

--- a/solution.py
+++ b/solution.py
@@ -13,7 +13,6 @@
 INNER = HEADS * HEAD
 GROUPS = 4
 WINDOW = 8
-AHEAD = 2
 LOG2E = 1.4426950408889634
 F32 = jnp.float32
 BF16 = jnp.bfloat16
@@ -49,7 +48,7 @@
     table_ref, x_ref, gate_ref, bc_ref, dt_ref, load_sem,
     got_x, got_bc, got_dt, y_send, got_y, f_send, got_f, t_send, got_t, s_send, got_s,
     l_send, got_l, i_send, got_i, e_send, got_e, w_row, u_row_s, end_s, near, acc, act, mixed,
-    x_out, x_in, m_out, m_in, y_out, y_in, f_out, f_in, s_out, s_in, l_out, l_in, i_out, i_in, e_out, e_in,
+    x_out, x_in, m_out, m_in, y_out, y_in, f_out, f_in, s_out, s_in, l_out, l_in, i_out, i_in, e_out, e_in, known,
 ):
     tile_rows = x_ref.shape[0]
     tokens = tile_rows * 8
@@ -84,9 +83,8 @@
         pl.semaphore_signal(barrier, inc=1, device_id=device, device_id_type=pl.DeviceIdType.MESH)
 
     near_set = sorted(set(to) | set(fro))
-    for d in near_set:
-        greet(col=around(me_col + d))
-    for c in (after, before, across):
+    greeted = [around(me_col + d) for d in near_set] + ([across] if windows > 2 else [])
+    for c in greeted:
         greet(col=c)
     for q in row_peers:
         greet(row=q)
@@ -157,23 +155,30 @@
     f_send[...] = states.astype(BF16).reshape(8, STATE, INNER)
     t_send[...] = jnp.concatenate([end_col, jnp.zeros((8, 128 - HEADS), F32)], axis=1)
 
+    def send_states():
+        for q in row_peers:
+            send_row(f_send.at[q], got_f.at[me_row], f_out.at[0], f_in.at[0], q)
+            send_row(t_send, got_t.at[me_row], f_out.at[1], f_in.at[1], q)
+
+    def send_small(d):
+        c = around(me_col + d)
+        send_col(bc_ref.at[rows_of(c)], got_bc.at[middle - d], m_out.at[0], m_in.at[0], c)
+        send_col(dt_ref.at[rows_of(c)], got_dt.at[middle - d], m_out.at[1], m_in.at[1], c)
+
     def send_tokens(g):
         part = pl.ds(g * group, group)
         for d in to:
             c = around(me_col + d)
             send_col(x_ref.at[rows_of(c), :, part], got_x.at[middle - d, :, :, part], x_out.at[g], x_in.at[g], c)
 
-    pl.semaphore_wait(barrier, len(near_set) + 3 + tall - 1)
+    pl.semaphore_wait(barrier, len(greeted) + tall - 1)
 
     for d in to:
-        c = around(me_col + d)
-        send_col(bc_ref.at[rows_of(c)], got_bc.at[middle - d], m_out.at[0], m_in.at[0], c)
-        send_col(dt_ref.at[rows_of(c)], got_dt.at[middle - d], m_out.at[1], m_in.at[1], c)
-    for g in range(AHEAD):
+        send_small(d)
+    send_states()
+    for g in range(GROUPS):
         send_tokens(g)
-    for q in row_peers:
-        send_row(f_send.at[q], got_f.at[me_row], f_out.at[0], f_in.at[0], q)
-        send_row(t_send, got_t.at[me_row], f_out.at[1], f_in.at[1], q)
+    pl.semaphore_signal(known, inc=1, device_id={"col": around(me_col - middle)}, device_id_type=pl.DeviceIdType.MESH)
     got_bc[middle] = bc_ref[rows_of(me_col)]
     got_dt[middle] = dt_ref[rows_of(me_col)]
     got_x[middle] = x_ref[rows_of(me_col)]
@@ -198,6 +203,7 @@
 
     wait_near(got_bc, m_in.at[0])
     wait_near(got_dt, m_in.at[1])
+    pl.semaphore_wait(known, 1)
     line_size = 8 * lines
     tile_i, tile_j = rows // line_size, cols // line_size
     line_i, line_j = (rows // 8) % lines, (cols // 8) % lines
@@ -254,8 +260,6 @@
             i_send[:, :, part] = state.reshape(lines, STATE, group).astype(BF16)
             pass_on(g)
 
-        if g + AHEAD < GROUPS:
-            send_tokens(g + AHEAD)
         for i in range(group_heads // 2):
             h = g * group_heads + 2 * i
             u_pair = u[:, i * 128 : i * 128 + 128]
@@ -399,7 +403,7 @@
     dma = pltpu.SemaphoreType.DMA
     out = pl.pallas_call(
         functools.partial(kernel, lanes, tall),
-        out_shape=jax.ShapeDtypeStruct((tile_rows, 8, INNER), BF16),
+        out_shape=pltpu.VMEM((tile_rows, 8, INNER), BF16),
         in_specs=[smem, hbm, vmem, vmem, vmem, hbm, hbm, hbm, hbm],
         out_specs=vmem,
         scratch_shapes=[
@@ -449,6 +453,7 @@
             dma((GROUPS,)),
             dma,
             dma,
+            pltpu.SemaphoreType.REGULAR,
         ],
         compiler_params=pltpu.CompilerParams(
             collective_id=0, has_side_effects=True, vmem_limit_bytes=60 * 1024 * 1024

time: 86.1 us -> 78.5 us (0.912)
  Pallas kernels: 82.8 us -> 76.7 us
  local copies, waits for them, and re-layouts: 2.06 us -> 0.88 us
    pallas_call x1, Pallas kernels: 82.8 us -> 76.7 us  [body(): pl.pallas_call(functools.partial(kernel, lanes, tall), out_shape=pltpu.VM...]
    unnamed x1, local copies, waits for them, and re-layouts: 2.06 us -> 0.88 us
where the time goes in v4:
time: 78.5 us; the launch traced here: 78.3 us
  Pallas kernels  76.7 us (98%)
  local copies, waits for them, and re-layouts  0.88 us (1%)
    pallas_call x1, Pallas kernels, body(): pl.pallas_call(functools.partial(kernel, lanes, tall), out_shape=pltpu.VM...  76.7 us

profile of v4, /device:TPU:6, one launch (start us, length us, event | category | flops | bytes accessed | tf_op | source)
XLA Modules:
  0.0 78.3 jit_solution(399135862508854905)
XLA Ops:
  0.7 76.7 %shard_map.91 = bf16[32,8,1536]{2,1,0:T(8,128)(2,1)S(1)} custom-call(s32[1]{0:T(128)S(6)} %copy.12.step_ref, f32[48,1000]{1,0:T(8,128)} %bitcast.11, f32[2,24]{1,0:T(2,128)} %rates_ref.1, f32[1,24]{1,0:T(1,128)} %bitcast.15, f32[12,128]{1,0:T(8,128)} %bitcast.14, bf16[32,8,1536]{2,1,0:T(8,128)(2,1)} %bitcast.9, bf16[32,8,1536]{2,1,0:T(8,128)(2,1)} %bitcast.10, ...), custom_call_target="tpu_custom_call" | custom-call | tf_op jit(solution)/shard_map/pallas_call | solution.py:404
  77.4 0.9 %copy.11 = bf16[1,32,8,1536]{3,2,1,0:T(8,128)(2,1)} copy(bf16[1,32,8,1536]{3,2,1,0:T(8,128)(2,1)S(1)} %bitcast.8) | data formatting | bytes 1572864

commit v5 on v4

--- a/solution.py
+++ b/solution.py
@@ -11,7 +11,7 @@
 HEAD = 64
 STATE = 16
 INNER = HEADS * HEAD
-GROUPS = 4
+GROUPS = 6
 WINDOW = 8
 LOG2E = 1.4426950408889634
 F32 = jnp.float32
@@ -57,7 +57,10 @@
     lines = tile_rows // WINDOW
     group = INNER // GROUPS
     group_heads = HEADS // GROUPS
-    middle = WINDOW // 2
+    reach = WINDOW // 2
+    flip = lax.axis_index("img") % 2
+    middle = reach - flip
+    sense = 1 - 2 * flip
     me_col = lax.axis_index("col")
     me_row = lax.axis_index("row")
 
@@ -65,14 +68,15 @@
         return (c + 2 * lanes) % lanes
 
     def rows_of(c):
-        return pl.ds(((c + middle) % WINDOW) * lines, lines)
-
-    order = sorted(range(1, middle + 1), reverse=True)
-    to = [d for k in order for d in ((k, -k) if k < middle else (k,))]
-    fro = [d for k in order for d in ((-k, k) if k < middle else (-k,))]
+        return pl.ds(((c + WINDOW - middle) % WINDOW) * lines, lines)
+
+    order = sorted(range(1, reach + 1), reverse=True)
+    offsets = [d for k in order for d in ((k, -k) if k < reach else (k,))]
+    to = [sense * d for d in offsets]
+    fro = [-sense * d for d in offsets]
     row_peers = [(me_row + k) % tall for k in range(1, tall)]
     after, before, across = around(me_col + WINDOW), around(me_col - WINDOW), around(me_col + 2 * WINDOW)
-    place = ((me_col + middle - 1) % lanes) // WINDOW
+    place = (around(me_col - middle + WINDOW - 1)) // WINDOW
     cut = around(middle - me_col)
     cut_in = jnp.where(place == 0, cut, WINDOW)
     cut_out = jnp.where(place == 0, cut, 0)
@@ -82,8 +86,7 @@
     def greet(**device):
         pl.semaphore_signal(barrier, inc=1, device_id=device, device_id_type=pl.DeviceIdType.MESH)
 
-    near_set = sorted(set(to) | set(fro))
-    greeted = [around(me_col + d) for d in near_set] + ([across] if windows > 2 else [])
+    greeted = [around(me_col + d) for k in order for d in (k, -k)] + ([across] if windows > 2 else [])
     for c in greeted:
         greet(col=c)
     for q in row_peers:
@@ -111,6 +114,31 @@
     def wait_for(ref, sem):
         pltpu.make_async_copy(ref, ref, sem).wait()
 
+    def send_states():
+        for q in row_peers:
+            send_row(f_send.at[q], got_f.at[me_row], f_out.at[0], f_in.at[0], q)
+            send_row(t_send, got_t.at[me_row], f_out.at[1], f_in.at[1], q)
+
+    def send_small(d):
+        c = around(me_col + d)
+        send_col(bc_ref.at[rows_of(c)], got_bc.at[middle - d], m_out.at[0], m_in.at[0], c)
+        send_col(dt_ref.at[rows_of(c)], got_dt.at[middle - d], m_out.at[1], m_in.at[1], c)
+
+    def send_tokens(g):
+        part = pl.ds(g * group, group)
+        for d in to:
+            c = around(me_col + d)
+            send_col(x_ref.at[rows_of(c), :, part], got_x.at[middle - d, :, :, part], x_out.at[g], x_in.at[g], c)
+
+    pl.semaphore_wait(barrier, len(greeted) + tall - 1)
+
+    for i in (0, 1, 3):
+        loads[i].wait()
+    for d in to:
+        send_small(d)
+    for g in range(GROUPS):
+        send_tokens(g)
+    pl.semaphore_signal(known, inc=1, device_id={"col": around(me_col - reach)}, device_id_type=pl.DeviceIdType.MESH)
     rows = lax.broadcasted_iota(jnp.int32, (tokens, tokens), 0)
     cols = lax.broadcasted_iota(jnp.int32, (tokens, tokens), 1)
     causal = rows >= cols
@@ -127,8 +155,7 @@
         ).astype(BF16)
         return jnp.where(kept, dot(v, fan), 0.0)
 
-    for i in range(4):
-        loads[i].wait()
+    loads[2].wait()
     chosen = (lax.broadcasted_iota(jnp.int32, (8, table_ref.shape[1]), 1) == step_ref[0]).astype(BF16)
     bias = sum(
         lax.dot_general(chosen, part, (((1,), (1,)), ((), ())), preferred_element_type=F32)
@@ -155,35 +182,12 @@
     f_send[...] = states.astype(BF16).reshape(8, STATE, INNER)
     t_send[...] = jnp.concatenate([end_col, jnp.zeros((8, 128 - HEADS), F32)], axis=1)
 
-    def send_states():
-        for q in row_peers:
-            send_row(f_send.at[q], got_f.at[me_row], f_out.at[0], f_in.at[0], q)
-            send_row(t_send, got_t.at[me_row], f_out.at[1], f_in.at[1], q)
-
-    def send_small(d):
-        c = around(me_col + d)
-        send_col(bc_ref.at[rows_of(c)], got_bc.at[middle - d], m_out.at[0], m_in.at[0], c)
-        send_col(dt_ref.at[rows_of(c)], got_dt.at[middle - d], m_out.at[1], m_in.at[1], c)
-
-    def send_tokens(g):
-        part = pl.ds(g * group, group)
-        for d in to:
-            c = around(me_col + d)
-            send_col(x_ref.at[rows_of(c), :, part], got_x.at[middle - d, :, :, part], x_out.at[g], x_in.at[g], c)
-
-    pl.semaphore_wait(barrier, len(greeted) + tall - 1)
-
-    for d in to:
-        send_small(d)
     send_states()
-    for g in range(GROUPS):
-        send_tokens(g)
-    pl.semaphore_signal(known, inc=1, device_id={"col": around(me_col - middle)}, device_id_type=pl.DeviceIdType.MESH)
+    got_f[me_row] = f_send[me_row]
+    got_t[me_row] = t_send[...]
     got_bc[middle] = bc_ref[rows_of(me_col)]
     got_dt[middle] = dt_ref[rows_of(me_col)]
     got_x[middle] = x_ref[rows_of(me_col)]
-    got_f[me_row] = f_send[me_row]
-    got_t[me_row] = t_send[...]
 
     def wait_near(ref, sem):
         wait_for(ref.at[pl.ds(0, WINDOW - 1)], sem)

time: 78.5 us -> 75.4 us (0.961)
  the two profiles are of different devices: /device:TPU:6 before, /device:TPU:1 now
where the time goes in v5:
time: 75.4 us; the launch traced here: 75.3 us
  Pallas kernels  73.7 us (98%)
  local copies, waits for them, and re-layouts  0.88 us (1%)
    pallas_call x1, Pallas kernels, body(): pl.pallas_call(functools.partial(kernel, lanes, tall), out_shape=pltpu.VM...  73.7 us

profile of v5, /device:TPU:1, one launch (start us, length us, event | category | flops | bytes accessed | tf_op | source)
XLA Modules:
  0.0 75.3 jit_solution(3405291982441864845)
XLA Ops:
  0.7 73.7 %shard_map.91 = bf16[32,8,1536]{2,1,0:T(8,128)(2,1)S(1)} custom-call(s32[1]{0:T(128)S(6)} %copy.12.step_ref, f32[48,1000]{1,0:T(8,128)} %bitcast.11, f32[2,24]{1,0:T(2,128)} %rates_ref.1, f32[1,24]{1,0:T(1,128)} %bitcast.15, f32[12,128]{1,0:T(8,128)} %bitcast.14, bf16[32,8,1536]{2,1,0:T(8,128)(2,1)} %bitcast.9, bf16[32,8,1536]{2,1,0:T(8,128)(2,1)} %bitcast.10, ...), custom_call_target="tpu_custom_call" | custom-call | tf_op jit(solution)/shard_map/pallas_call | solution.py:408
  74.4 0.9 %copy.11 = bf16[1,32,8,1536]{3,2,1,0:T(8,128)(2,1)} copy(bf16[1,32,8,1536]{3,2,1,0:T(8,128)(2,1)S(1)} %bitcast.8) | data formatting | bytes 1572864

commit v6 on v5

--- a/solution.py
+++ b/solution.py
@@ -13,6 +13,7 @@
 INNER = HEADS * HEAD
 GROUPS = 6
 WINDOW = 8
+LAG = 3
 LOG2E = 1.4426950408889634
 F32 = jnp.float32
 BF16 = jnp.bfloat16
@@ -344,20 +345,18 @@
             acc[:half, part] = jnp.where(lane < HEAD, dot(top0, u[:half]), dot(top1, u[:half])) + kept[:half]
             acc[half:, part] = jnp.where(lane < HEAD, dot(low0, u), dot(low1, u)) + kept[half:]
 
-    for g in range(2, GROUPS):
-        enter(g)
-        if g == 2:
-            column_local()
-    if GROUPS <= 2:
-        column_local()
-
     wait_for(got_e, e_in)
     before_decay = expand(got_e[:lines, :HEADS], spread, 3)
-    second(0)
-    for g in range(GROUPS):
-        if g + 1 < GROUPS:
-            second(g + 1)
-        finish(g, before_decay)
+
+    for turn in range(2, GROUPS + LAG + 1):
+        if turn < GROUPS:
+            enter(turn)
+        if turn == 2:
+            column_local()
+        if 0 <= turn - LAG < GROUPS:
+            second(turn - LAG)
+        if 0 <= turn - LAG - 1 < GROUPS:
+            finish(turn - LAG - 1, before_decay)
 
     loads[4].wait()
     gate = gate_ref[...].astype(F32).reshape(tokens, INNER)

time: 75.4 us -> 78 us (1.034)
  the two profiles are of different devices: /device:TPU:1 before, /device:TPU:6 now
where the time goes in v6:
time: 78 us; the launch traced here: 77.1 us
  Pallas kernels  75.6 us (97%)
  local copies, waits for them, and re-layouts  0.88 us (1%)
    pallas_call x1, Pallas kernels, body(): pl.pallas_call(functools.partial(kernel, lanes, tall), out_shape=pltpu.VM...  75.6 us

profile of v6, /device:TPU:6, one launch (start us, length us, event | category | flops | bytes accessed | tf_op | source)
XLA Modules:
  0.0 77.1 jit_solution(6542435211625243446)
XLA Ops:
  0.7 75.6 %shard_map.91 = bf16[32,8,1536]{2,1,0:T(8,128)(2,1)S(1)} custom-call(s32[1]{0:T(128)S(6)} %copy.12.step_ref, f32[48,1000]{1,0:T(8,128)} %bitcast.11, f32[2,24]{1,0:T(2,128)} %rates_ref.1, f32[1,24]{1,0:T(1,128)} %bitcast.15, f32[12,128]{1,0:T(8,128)} %bitcast.14, bf16[32,8,1536]{2,1,0:T(8,128)(2,1)} %bitcast.9, bf16[32,8,1536]{2,1,0:T(8,128)(2,1)} %bitcast.10, ...), custom_call_target="tpu_custom_call" | custom-call | tf_op jit(solution)/shard_map/pallas_call | solution.py:407
  76.2 0.9 %copy.11 = bf16[1,32,8,1536]{3,2,1,0:T(8,128)(2,1)} copy(bf16[1,32,8,1536]{3,2,1,0:T(8,128)(2,1)S(1)} %bitcast.8) | data formatting | bytes 1572864
